TPU v7x, 1024 devices: a whole 8x8x8 slice. The times are simulated.
1024 devices in a mesh: row: 32 (over y, z_lo), col: 32 (over x, z_hi, core).
Axes of the slice: x: 8, y: 8, z: 8 (z_hi: 2, z_lo: 4; z = z_hi * 4 + z_lo), core: 2. Of those that a mesh axis runs over, the one named last changes fastest.
Arguments:
- spectra: bfloat16 [600, 128, 4096], P(None, 'row', 'col'), may hold values from 0.0099487305 to 1
- wind: float32 [2, 128, 4096], P(None, 'row', 'col'), may hold values from -18 to 18
- wave_current: float32 [3, 128, 4096], P(None, 'row', 'col'), may hold values from -3 to 3
- wave_wet: int32 [128, 4096], P('row', 'col'), may hold values 0 or 1
- interaction: bfloat16 [600, 600], replicated, may hold values from -0.25 to 0.25
- input_rate: float32 [25], replicated, may hold values from 0.002 to 0.03
- eta_gain: float32 [25], replicated, may hold values from -0.5 to 0.5
- stress_map: float32 [2, 600], replicated, may hold values from -0.25 to 0.25
- stokes_map: float32 [6, 600], replicated, may hold values from -0.25 to 0.25
- ocean_vel: float32 [2, 30, 256, 4096], P(None, None, 'row', 'col'), may hold values from -3 to 3
- ocean_eta: float32 [256, 4096], P('row', 'col'), may hold values from -3 to 3
- ocean_wet: int32 [256, 4096], P('row', 'col'), may hold values 0 or 1
- coriolis: float32 [256, 4096], P('row', 'col'), may hold values from -1.5 to 1.5
- tau_profile: float32 [30], replicated, may hold values from 0.05 to 1
- stokes_profile: float32 [3, 30], replicated, may hold values from 0.05 to 1
- thickness: float32 [30], replicated, may hold values from 0.02 to 0.1
- mix_inverse: float32 [30, 30], replicated
- fold_index: int32 [4096], P('col'), may hold values from 0 to 4095, as said below
- wave_send: int32 [32, 32, 3, 64], P('row', 'col'), may hold values from 0 to 511
- ocean_recv: bfloat16 [32, 32, 3, 64, 1024], P('row', 'col'), may hold values from -0.4375 to 0.4375
- ocean_send: int32 [32, 32, 3, 64], P('row', 'col'), may hold values from 0 to 1023
- wave_recv: bfloat16 [32, 32, 3, 64, 512], P('row', 'col'), may hold values from -0.4375 to 0.4375
Outputs:
- spectra_out: bfloat16 [600, 128, 4096], P(None, 'row', 'col')
- ocean_vel_out: float32 [2, 30, 256, 4096], P(None, None, 'row', 'col')
- ocean_eta_out: float32 [256, 4096], P('row', 'col')
- current_out: float32 [3, 128, 4096], P(None, 'row', 'col')
Inputs may be any that keep to these rules, and one draw needn't show every extreme that they name: `wave_send`: entries name cells of the sending wave tile numbered y * 128 + x. `ocean_send`: entries name cells of the sending ocean tile numbered y * 128 + x. `fold_index`: each entry names a column of the whole top line; columns of any block may be named from any block.
All inputs are finite; a program needn't handle non-finite values. No bound on the sum of `wave_wet` or of `ocean_wet` on one device may be relied on, other than what follows from the above.
Results may differ from a plain program's by a relative error of at most 0.006.
Values may be sent and summed in bfloat16 or wider, within the bound.
A program may use at most 32 MiB of HBM per device.

v0:
```python
import math

import jax
import jax.numpy as jnp
from jax import lax
from jax.sharding import PartitionSpec as P

NDIR = 24
NBAND = 3
STEPS = 2


viscous = 0.2
surface_rate = 0.5
highest = lax.Precision.HIGHEST


def extended(array, sides, width):
    edges = {}
    for axis, dim in sides:
        peers, length = (lax.axis_size(axis), array.shape[dim])
        up = [(i, (i + 1) % peers) for i in range(peers)]
        last = lax.slice_in_dim(array, length - width, length, axis=dim)
        initial = lax.slice_in_dim(array, 0, width, axis=dim)
        edges[dim] = (
            lax.ppermute(last, axis, up),
            lax.ppermute(initial, axis, [(b, a) for a, b in up]),
        )
    done = []
    for _, dim in sides:
        low, high = edges[dim]
        around = [(width, width) if d in done else (0, 0) for d in range(array.ndim)]
        array = jnp.concatenate([jnp.pad(low, around), array, jnp.pad(high, around)], axis=dim)
        done.append(dim)
    return array


def joined_along(tiles, dim):
    tiles = jnp.moveaxis(tiles, 0, dim)
    dims = tiles.shape
    return tiles.reshape(*dims[:dim], dims[dim] * dims[dim + 1], *dims[dim + 2 :])


def copy_for_each(array, axis):
    copies = jnp.broadcast_to(array, (lax.axis_size(axis), *array.shape))
    return lax.all_to_all(copies, axis, split_axis=0, concat_axis=0, tiled=True)


def collect(array, axis, dim):
    return joined_along(copy_for_each(array, axis), dim)


def padded_2(array, sides, width):
    for axis, dim in sides:
        peers, length = (lax.axis_size(axis), array.shape[dim])
        up = [(i, (i + 1) % peers) for i in range(peers - 1)]
        down = [(j, i) for i, j in up]
        last = lax.slice_in_dim(array, length - width, length, axis=dim)
        initial = lax.slice_in_dim(array, 0, width, axis=dim)
        before = lax.ppermute(last, axis, up)
        after = lax.ppermute(initial, axis, down)
        array = jnp.concatenate([before, array, after], axis=dim)
    return array


def wave_cells(
    energy,
    wind_cells,
    current,
    wet_cells,
    interaction,
    input_rate,
    eta_gain,
    stress_map,
    stokes_map,
):
    spectrum_len = energy.shape[0]
    heading = ((jnp.arange(spectrum_len) % NDIR).astype(jnp.float32) + 0.5) * (2.0 * math.pi / NDIR)
    cosine = jnp.cos(heading)[:, None]
    sine_dir = jnp.sin(heading)[:, None]
    relative = (wind_cells[0] - current[0]) * cosine + (wind_cells[1] - current[1]) * sine_dir
    growth = jnp.repeat(input_rate, NDIR)[:, None] * jax.nn.softplus(relative)
    energy_wide = energy.astype(jnp.float32)
    transfer_term = jnp.dot(interaction, energy, preferred_element_type=jnp.float32)
    level_term = jnp.repeat(eta_gain, NDIR)[:, None] * current[2]
    updated = (
        wet_cells.astype(jnp.float32)
        * (energy_wide + (growth + level_term) * energy_wide + transfer_term)
    ).astype(jnp.bfloat16)
    stress = jnp.dot(stress_map, growth * energy_wide, precision=highest)
    stokes = jnp.dot(stokes_map, updated.astype(jnp.float32), precision=highest)
    return (updated, jnp.concatenate([stress, stokes], 0).astype(jnp.bfloat16))


def ocean_force(velocity, forcing, ocean_wet, coriolis, tau_profile, stokes_profile):
    wet_mask = ocean_wet.astype(jnp.float32)
    along_u = tau_profile[:, None, None] * forcing[0]
    along_v = tau_profile[:, None, None] * forcing[1]
    for band_index in range(NBAND):
        profile = stokes_profile[band_index][:, None, None]
        along_u = along_u + coriolis * profile * forcing[3 + 2 * band_index]
        along_v = along_v - coriolis * profile * forcing[2 + 2 * band_index]
    return wet_mask * (velocity + jnp.stack([along_u, along_v]))


def ocean_finish(forced, padded, elevation, ocean_wet, thickness, mix_inverse):
    wet_mask = ocean_wet.astype(jnp.float32)
    laplacian = (
        padded[:, :, 2:, 1:-1]
        + padded[:, :, :-2, 1:-1]
        + padded[:, :, 1:-1, 2:]
        + padded[:, :, 1:-1, :-2]
        - 4.0 * forced
    )
    smoothed = wet_mask * (forced + viscous * laplacian)
    transport = jnp.einsum("l,clyx->cyx", thickness, padded, precision=highest)
    divergence = 0.5 * (transport[0, 1:-1, 2:] - transport[0, 1:-1, :-2]) + 0.5 * (
        transport[1, 2:, 1:-1] - transport[1, :-2, 1:-1]
    )
    eta_next = wet_mask * (elevation - surface_rate * divergence)
    vel_next = jnp.einsum("lm,cmyx->clyx", mix_inverse, smoothed, precision=highest)
    return (vel_next, eta_next)


def edge_cells(forced, fold_index):
    padded = extended(forced.astype(jnp.bfloat16), (("row", 2), ("col", 3)), 1).astype(forced.dtype)
    row_count = lax.axis_size("row")
    row_here = lax.axis_index("row")
    top_line = forced[:, :, -1, :]
    whole_line = collect(top_line, "col", 2)
    across = -jnp.take(whole_line, fold_index, axis=2)
    north_row = jnp.where(row_here == row_count - 1, across, padded[:, :, -1, 1:-1])
    south_row = jnp.where(row_here == 0, 0.0, padded[:, :, 0, 1:-1])
    return padded.at[:, :, -1, 1:-1].set(north_row).at[:, :, 0, 1:-1].set(south_row)


def route_fields(fields, send_rows, weights, toward_ocean):
    slot_rows = jnp.moveaxis(jnp.take(fields, send_rows, axis=1), 1, 0)
    outgoing = jnp.stack([slot_rows[0], slot_rows[2]])
    if toward_ocean:
        margined = padded_2(outgoing, (("row", 0),), 1)
    else:
        margined = padded_2(outgoing, (("row", 0),), 1)
    from_south = margined[0]
    from_north = margined[3]
    received = jnp.stack([from_north, slot_rows[1], from_south])
    return jnp.einsum("jfs,jsn->fn", received, weights, preferred_element_type=jnp.float32)


def shards(
    spectra,
    wind,
    wave_current,
    wave_wet,
    interaction,
    input_rate,
    eta_gain,
    stress_map,
    stokes_map,
    ocean_vel,
    ocean_eta,
    ocean_wet,
    coriolis,
    tau_profile,
    stokes_profile,
    thickness,
    mix_inverse,
    fold_index,
    wave_send,
    ocean_recv,
    ocean_send,
    wave_recv,
):
    spectrum_len, wave_rows, wave_cols = spectra.shape
    cell_count = wave_rows * wave_cols
    ocean_rows, ocean_cols = ocean_eta.shape
    energy = spectra.reshape(spectrum_len, cell_count)
    wind_cells = wind.reshape(2, cell_count)
    current = wave_current.reshape(3, cell_count)
    wet_cells = wave_wet.reshape(cell_count)
    velocity = ocean_vel
    elevation = ocean_eta
    for step_index in range(STEPS):
        energy, fields = wave_cells(
            energy,
            wind_cells,
            current,
            wet_cells,
            interaction,
            input_rate,
            eta_gain,
            stress_map,
            stokes_map,
        )
        forcing = route_fields(fields, wave_send[0, 0], ocean_recv[0, 0], True).reshape(
            -1, ocean_rows, ocean_cols
        )
        forced = ocean_force(velocity, forcing, ocean_wet, coriolis, tau_profile, stokes_profile)
        padded = edge_cells(forced, fold_index)
        velocity, elevation = ocean_finish(
            forced, padded, elevation, ocean_wet, thickness, mix_inverse
        )
        back = (
            jnp.stack([velocity[0, 0], velocity[1, 0], elevation])
            .reshape(3, ocean_rows * ocean_cols)
            .astype(jnp.bfloat16)
        )
        current = route_fields(back, ocean_send[0, 0], wave_recv[0, 0], False)
    return (
        energy.reshape(spectrum_len, wave_rows, wave_cols),
        velocity,
        elevation,
        current.reshape(3, wave_rows, wave_cols),
    )


def solution(mesh):
    in_specs = (
        P(None, "row", "col"),
        P(None, "row", "col"),
        P(None, "row", "col"),
        P("row", "col"),
        P(),
        P(),
        P(),
        P(),
        P(),
        P(None, None, "row", "col"),
        P("row", "col"),
        P("row", "col"),
        P("row", "col"),
        P(),
        P(),
        P(),
        P(),
        P("col"),
        P("row", "col", None, None),
        P("row", "col", None, None, None),
        P("row", "col", None, None),
        P("row", "col", None, None, None),
    )
    out_specs = (
        P(None, "row", "col"),
        P(None, None, "row", "col"),
        P("row", "col"),
        P(None, "row", "col"),
    )
    return jax.shard_map(shards, mesh=mesh, in_specs=in_specs, out_specs=out_specs, check_vma=False)
```

profile of v0, /device:TPU:65, one launch (start us, length us, event | category | flops | bytes accessed | tf_op | source)
XLA Modules:
  0.0 191.0 jit_solution(16941895033457964104)
XLA Ops:
  5.2 2.8 %fusion.13 = bf16[2,512]{1,0:T(2,128)(2,1)S(1)} fusion(f32[2,600]{1,0:T(2,128)} %param.43, f32[600]{0:T(1024)S(1)} %get-tuple-element.134, f32[512]{0:T(512)S(1)} %get-tuple-element.102, f32[600]{0:T(1024)S(1)} %get-tuple-element.135, f32[512]{0:T(512)S(1)} %get-tuple-element.101, f32[600]{0:T(1024)S(1)} %mul.659, bf16[75,8,4,128]{3,2,1,0:T(4,128)(2,1)} %bitcast.265), kind=kOutput, calls=%fused_computation.35 | convolution fusion | flops 11060224 | bytes 632544 | tf_op jit(solution)/shard_map/dot_general | solution.py:90
  12.0 10.1 %collective-permute-start = (bf16[1,8,64]{2,1,0:T(8,128)(2,1)S(1)}, bf16[1,8,64]{2,1,0:T(8,128)(2,1)S(1)}, u32[]{:S(2)}, u32[]{:S(2)}) collective-permute-start(bf16[1,8,64]{2,1,0:T(8,128)(2,1)S(1)} %get-tuple-element.113), channel_id=1, source_target_pairs={{32,0},{64,32},{96,64},{128,96},{160,128},{192,160},{224,192},{256... | collective-permute-start | bytes 3080 | tf_op jit(solution)/shard_map/ppermute | solution.py:61
  24.1 6.2 %collective-permute-done.1 = bf16[1,8,64]{2,1,0:T(8,128)(2,1)S(1)} collective-permute-done((bf16[1,8,64]{2,1,0:T(8,128)(2,1)S(1)}, bf16[1,8,64]{2,1,0:T(8,128)(2,1)S(1)}, u32[]{:S(2)}, u32[]{:S(2)}) %collective-permute-start.1) | collective-permute-done | bytes 1056 | tf_op jit(solution)/shard_map/ppermute | solution.py:60
  32.1 18.5 %all-to-all-start = ((f32[32,2,30,128]{3,1,2,0:T(2,128)}), f32[32,2,30,128]{3,1,2,0:T(2,128)S(1)}, u32[]{:S(2)}, u32[]{:S(2)}) async-start(f32[32,2,30,128]{3,1,2,0:T(2,128)} %broadcast_in_dim.42), calls=%async_computation | async-start | bytes 1966080 | tf_op jit(solution)/shard_map/all_to_all | solution.py:46
  52.1 7.4 %collective-permute-start.2 = (bf16[2,30,8,1]{3,1,2,0:T(8,128)(2,1)S(1)}, bf16[2,30,8,1]{3,1,2,0:T(8,128)(2,1)S(1)}, u32[]{:S(2)}, u32[]{:S(2)}) collective-permute-start(bf16[2,30,8,1]{3,1,2,0:T(8,128)(2,1)S(1)} %get-tuple-element.83), channel_id=1, source_target_pairs={{0,1},{1,2},{2,3},{3,4},{4,5},{5,6},{6,7},{7,8},{8,9},{9,10},{10,1... | collective-permute-start | bytes 2888 | tf_op jit(solution)/shard_map/ppermute | solution.py:26
  63.4 7.3 %collective-permute-start.4 = (bf16[2,30,1,128]{3,1,2,0:T(8,128)(2,1)S(1)}, bf16[2,30,1,128]{3,1,2,0:T(8,128)(2,1)S(1)}, u32[]{:S(2)}, u32[]{:S(2)}) collective-permute-start(bf16[2,30,1,128]{3,1,2,0:T(8,128)(2,1)S(1)} %get-tuple-element.82), channel_id=1, source_target_pairs={{32,0},{64,32},{96,64},{128,96},{160,128},{192,160},{224,192},{256... | collective-permute-start | bytes 46088 | tf_op jit(solution)/shard_map/ppermute | solution.py:27
  70.7 5.9 %collective-permute-done.2 = bf16[2,30,8,1]{3,1,2,0:T(8,128)(2,1)S(1)} collective-permute-done((bf16[2,30,8,1]{3,1,2,0:T(8,128)(2,1)S(1)}, bf16[2,30,8,1]{3,1,2,0:T(8,128)(2,1)S(1)}, u32[]{:S(2)}, u32[]{:S(2)}) %collective-permute-start.2) | collective-permute-done | bytes 992 | tf_op jit(solution)/shard_map/ppermute | solution.py:26
  76.6 2.0 %collective-permute-done.5 = bf16[2,30,8,1]{3,1,2,0:T(8,128)(2,1)S(1)} collective-permute-done((bf16[2,30,8,1]{3,1,2,0:T(8,128)(2,1)S(1)}, bf16[2,30,8,1]{3,1,2,0:T(8,128)(2,1)S(1)}, u32[]{:S(2)}, u32[]{:S(2)}) %collective-permute-start.5) | collective-permute-done | bytes 992 | tf_op jit(solution)/shard_map/ppermute | solution.py:27
  80.1 4.4 %copy.110 = f32[2,30,32,128]{1,0,3,2:T(2,128)} copy(f32[2,30,32,128]{3,0,1,2:T(2,128)S(1)} %bitcast.232) | data formatting | bytes 1966080 | tf_op jit(solution)/shard_map/reshape | solution.py:41
  84.5 3.0 %gather_fusion.1 = f32[128,2,30]{2,1,0:T(2,128)S(1)} fusion(f32[2,30,4096]{1,0,2:T(2,128)} %bitcast.231, s32[1024]{0:T(1024)S(1)} %pad_clamp_fusion.1), kind=kCustom, calls=%fused_computation.1.clone | custom fusion | bytes 61952 | tf_op jit(solution)/shard_map/jit(_take)/gather | solution.py:131
  93.3 4.0 %collective-permute-start.6 = (bf16[1,3,64]{2,1,0:T(4,128)(2,1)S(1)}, bf16[1,3,64]{2,1,0:T(4,128)(2,1)S(1)}, u32[]{:S(2)}, u32[]{:S(2)}) collective-permute-start(bf16[1,3,64]{2,1,0:T(4,128)(2,1)S(1)} %get-tuple-element.122), channel_id=1, source_target_pairs={{32,0},{64,32},{96,64},{128,96},{160,128},{192,160},{224,192},{256... | collective-permute-start | bytes 1160 | tf_op jit(solution)/shard_map/ppermute | solution.py:61
  97.3 2.1 %collective-permute-start.7 = (bf16[1,3,64]{2,1,0:T(4,128)(2,1)S(1)}, bf16[1,3,64]{2,1,0:T(4,128)(2,1)S(1)}, u32[]{:S(2)}, u32[]{:S(2)}) collective-permute-start(bf16[1,3,64]{2,1,0:T(4,128)(2,1)S(1)} %get-tuple-element.123), channel_id=1, source_target_pairs={{0,32},{32,64},{64,96},{96,128},{128,160},{160,192},{192,224},{224... | collective-permute-start | bytes 1160 | tf_op jit(solution)/shard_map/ppermute | solution.py:60
  99.5 6.1 %collective-permute-done.7 = bf16[1,3,64]{2,1,0:T(4,128)(2,1)S(1)} collective-permute-done((bf16[1,3,64]{2,1,0:T(4,128)(2,1)S(1)}, bf16[1,3,64]{2,1,0:T(4,128)(2,1)S(1)}, u32[]{:S(2)}, u32[]{:S(2)}) %collective-permute-start.7) | collective-permute-done | bytes 416 | tf_op jit(solution)/shard_map/ppermute | solution.py:60
  112.5 3.4 %collective-permute-start.9 = (bf16[1,8,64]{2,1,0:T(8,128)(2,1)S(1)}, bf16[1,8,64]{2,1,0:T(8,128)(2,1)S(1)}, u32[]{:S(2)}, u32[]{:S(2)}) collective-permute-start(bf16[1,8,64]{2,1,0:T(8,128)(2,1)S(1)} %get-tuple-element.109), channel_id=1, source_target_pairs={{0,32},{32,64},{64,96},{96,128},{128,160},{160,192},{192,224},{224... | collective-permute-start | bytes 3080 | tf_op jit(solution)/shard_map/ppermute | solution.py:60
  115.9 4.9 %collective-permute-done.9 = bf16[1,8,64]{2,1,0:T(8,128)(2,1)S(1)} collective-permute-done((bf16[1,8,64]{2,1,0:T(8,128)(2,1)S(1)}, bf16[1,8,64]{2,1,0:T(8,128)(2,1)S(1)}, u32[]{:S(2)}, u32[]{:S(2)}) %collective-permute-start.9) | collective-permute-done | bytes 1056 | tf_op jit(solution)/shard_map/ppermute | solution.py:60
  122.5 11.5 %all-to-all-start.1 = ((f32[32,2,30,128]{3,1,2,0:T(2,128)}), f32[32,2,30,128]{3,1,2,0:T(2,128)S(1)}, u32[]{:S(2)}, u32[]{:S(2)}) async-start(f32[32,2,30,128]{3,1,2,0:T(2,128)} %broadcast_in_dim.44), calls=%async_computation.1 | async-start | bytes 1966080 | tf_op jit(solution)/shard_map/all_to_all | solution.py:46
  135.9 7.3 %collective-permute-start.12 = (bf16[2,30,1,128]{3,1,0,2:T(8,128)(2,1)S(1)}, bf16[2,30,1,128]{3,1,0,2:T(8,128)(2,1)S(1)}, u32[]{:S(2)}, u32[]{:S(2)}) collective-permute-start(bf16[2,30,1,128]{3,1,0,2:T(8,128)(2,1)S(1)} %get-tuple-element.76), channel_id=1, source_target_pairs={{32,0},{64,32},{96,64},{128,96},{160,128},{192,160},{224,192},{256... | collective-permute-start | bytes 46088 | tf_op jit(solution)/shard_map/ppermute | solution.py:27
  143.3 8.0 %collective-permute-start.10 = (bf16[2,30,8,1]{3,1,0,2:T(8,128)(2,1)S(1)}, bf16[2,30,8,1]{3,1,0,2:T(8,128)(2,1)S(1)}, u32[]{:S(2)}, u32[]{:S(2)}) collective-permute-start(bf16[2,30,8,1]{3,1,0,2:T(8,128)(2,1)S(1)} %get-tuple-element.77), channel_id=1, source_target_pairs={{0,1},{1,2},{2,3},{3,4},{4,5},{5,6},{6,7},{7,8},{8,9},{9,10},{10,1... | collective-permute-start | bytes 2888 | tf_op jit(solution)/shard_map/ppermute | solution.py:26
  153.3 9.3 %collective-permute-done.10 = bf16[2,30,8,1]{3,1,0,2:T(8,128)(2,1)S(1)} collective-permute-done((bf16[2,30,8,1]{3,1,0,2:T(8,128)(2,1)S(1)}, bf16[2,30,8,1]{3,1,0,2:T(8,128)(2,1)S(1)}, u32[]{:S(2)}, u32[]{:S(2)}) %collective-permute-start.10) | collective-permute-done | bytes 992 | tf_op jit(solution)/shard_map/ppermute | solution.py:26
  162.6 2.8 %collective-permute-done.13 = bf16[2,30,8,1]{3,1,0,2:T(8,128)(2,1)S(1)} collective-permute-done((bf16[2,30,8,1]{3,1,0,2:T(8,128)(2,1)S(1)}, bf16[2,30,8,1]{3,1,0,2:T(8,128)(2,1)S(1)}, u32[]{:S(2)}, u32[]{:S(2)}) %collective-permute-start.13) | collective-permute-done | bytes 992 | tf_op jit(solution)/shard_map/ppermute | solution.py:27
  165.8 4.4 %copy.115 = f32[2,30,32,128]{1,0,3,2:T(2,128)} copy(f32[2,30,32,128]{3,0,1,2:T(2,128)S(1)} %bitcast.233) | data formatting | bytes 1966080 | tf_op jit(solution)/shard_map/reshape | solution.py:41
  170.2 3.1 %gather_fusion.4 = f32[128,2,30]{2,1,0:T(2,128)S(1)} fusion(f32[2,30,4096]{1,0,2:T(2,128)} %bitcast.230, s32[1024]{0:T(1024)} %copy-done.20), kind=kCustom, calls=%fused_computation.4.clone | custom fusion | bytes 61952 | tf_op jit(solution)/shard_map/jit(_take)/gather | solution.py:131
  181.7 3.4 %collective-permute-start.15 = (bf16[1,3,64]{2,1,0:T(4,128)(2,1)S(1)}, bf16[1,3,64]{2,1,0:T(4,128)(2,1)S(1)}, u32[]{:S(2)}, u32[]{:S(2)}) collective-permute-start(bf16[1,3,64]{2,1,0:T(4,128)(2,1)S(1)} %get-tuple-element.120), channel_id=1, source_target_pairs={{0,32},{32,64},{64,96},{96,128},{128,160},{160,192},{192,224},{224... | collective-permute-start | bytes 1160 | tf_op jit(solution)/shard_map/ppermute | solution.py:60
  186.9 3.3 %collective-permute-done.15 = bf16[1,3,64]{2,1,0:T(4,128)(2,1)S(1)} collective-permute-done((bf16[1,3,64]{2,1,0:T(4,128)(2,1)S(1)}, bf16[1,3,64]{2,1,0:T(4,128)(2,1)S(1)}, u32[]{:S(2)}, u32[]{:S(2)}) %collective-permute-start.15) | collective-permute-done | bytes 416 | tf_op jit(solution)/shard_map/ppermute | solution.py:60
  (228 shorter events, 48.0 us)
Async XLA Ops:
  8.2 22.2 %copy-start.1 = (bf16[1,1,3,64,1024]{4,3,2,1,0:T(8,128)(2,1)S(1)}, bf16[1,1,3,64,1024]{4,3,2,1,0:T(8,128)(2,1)}, u32[]{:S(2)}) copy-start(bf16[1,1,3,64,1024]{4,3,2,1,0:T(8,128)(2,1)} %param.55) | copy-start | bytes 1179652
  10.4 20.2 %copy-start.44 = (f32[30]{0:T(128)S(1)}, f32[30]{0:T(128)}, u32[]{:S(2)}) copy-start(f32[30]{0:T(128)} %param.49) | copy-start | bytes 364
  10.4 20.3 %copy-start.6 = (f32[2,30,8,128]{3,2,1,0:T(8,128)S(1)}, f32[2,30,8,128]{3,2,1,0:T(8,128)}, u32[]{:S(2)}) copy-start(f32[2,30,8,128]{3,2,1,0:T(8,128)} %param.45) | copy-start | bytes 737284
  12.0 12.1 %collective-permute-start = (bf16[1,8,64]{2,1,0:T(8,128)(2,1)S(1)}, bf16[1,8,64]{2,1,0:T(8,128)(2,1)S(1)}, u32[]{:S(2)}, u32[]{:S(2)}) collective-permute-start(bf16[1,8,64]{2,1,0:T(8,128)(2,1)S(1)} %get-tuple-element.113), channel_id=1, source_target_pairs={{32,0},{64,32},{96,64},{128,96},{160,128},{192,160},{224,192},{256... | collective-permute-start | bytes 3080 | tf_op jit(solution)/shard_map/ppermute | solution.py:61
  22.1 8.2 %collective-permute-start.1 = (bf16[1,8,64]{2,1,0:T(8,128)(2,1)S(1)}, bf16[1,8,64]{2,1,0:T(8,128)(2,1)S(1)}, u32[]{:S(2)}, u32[]{:S(2)}) collective-permute-start(bf16[1,8,64]{2,1,0:T(8,128)(2,1)S(1)} %get-tuple-element.114), channel_id=1, source_target_pairs={{0,32},{32,64},{64,96},{96,128},{128,160},{160,192},{192,224},{224... | collective-permute-start | bytes 3080 | tf_op jit(solution)/shard_map/ppermute | solution.py:60
  32.1 48.0 %all-to-all-start = ((f32[32,2,30,128]{3,1,2,0:T(2,128)}), f32[32,2,30,128]{3,1,2,0:T(2,128)S(1)}, u32[]{:S(2)}, u32[]{:S(2)}) async-start(f32[32,2,30,128]{3,1,2,0:T(2,128)} %broadcast_in_dim.42), calls=%async_computation | async-start | bytes 1966080 | tf_op jit(solution)/shard_map/all_to_all | solution.py:46
  50.8 33.7 %copy-start.20 = (s32[1024]{0:T(1024)}, s32[1024]{0:T(1024)S(1)}, u32[]{:S(2)}) copy-start(s32[1024]{0:T(1024)S(1)} %pad_clamp_fusion.1) | copy-start | bytes 12292
  52.0 41.3 %copy-start.30 = (pred[3,64]{1,0:T(4,128)(4,1)}, pred[3,64]{1,0:T(4,128)(4,1)S(1)}, u32[]{:S(2)}) copy-start(pred[3,64]{1,0:T(4,128)(4,1)S(1)} %compare_and_fusion) | copy-start | bytes 580
  52.1 24.5 %collective-permute-start.2 = (bf16[2,30,8,1]{3,1,2,0:T(8,128)(2,1)S(1)}, bf16[2,30,8,1]{3,1,2,0:T(8,128)(2,1)S(1)}, u32[]{:S(2)}, u32[]{:S(2)}) collective-permute-start(bf16[2,30,8,1]{3,1,2,0:T(8,128)(2,1)S(1)} %get-tuple-element.83), channel_id=1, source_target_pairs={{0,1},{1,2},{2,3},{3,4},{4,5},{5,6},{6,7},{7,8},{8,9},{9,10},{10,1... | collective-permute-start | bytes 2888 | tf_op jit(solution)/shard_map/ppermute | solution.py:26
  59.5 19.0 %collective-permute-start.5 = (bf16[2,30,8,1]{3,1,2,0:T(8,128)(2,1)S(1)}, bf16[2,30,8,1]{3,1,2,0:T(8,128)(2,1)S(1)}, u32[]{:S(2)}, u32[]{:S(2)}) collective-permute-start(bf16[2,30,8,1]{3,1,2,0:T(8,128)(2,1)S(1)} %get-tuple-element.84), channel_id=1, source_target_pairs={{1,0},{2,1},{3,2},{4,3},{5,4},{6,5},{7,6},{8,7},{9,8},{10,9},{11,1... | collective-permute-start | bytes 2888 | tf_op jit(solution)/shard_map/ppermute | solution.py:27
  61.5 17.1 %collective-permute-start.3 = (bf16[2,30,1,128]{3,1,2,0:T(8,128)(2,1)S(1)}, bf16[2,30,1,128]{3,1,2,0:T(8,128)(2,1)S(1)}, u32[]{:S(2)}, u32[]{:S(2)}) collective-permute-start(bf16[2,30,1,128]{3,1,2,0:T(8,128)(2,1)S(1)} %get-tuple-element.81), channel_id=1, source_target_pairs={{0,32},{32,64},{64,96},{96,128},{128,160},{160,192},{192,224},{224... | collective-permute-start | bytes 46088 | tf_op jit(solution)/shard_map/ppermute | solution.py:26
  63.4 15.1 %collective-permute-start.4 = (bf16[2,30,1,128]{3,1,2,0:T(8,128)(2,1)S(1)}, bf16[2,30,1,128]{3,1,2,0:T(8,128)(2,1)S(1)}, u32[]{:S(2)}, u32[]{:S(2)}) collective-permute-start(bf16[2,30,1,128]{3,1,2,0:T(8,128)(2,1)S(1)} %get-tuple-element.82), channel_id=1, source_target_pairs={{32,0},{64,32},{96,64},{128,96},{160,128},{192,160},{224,192},{256... | collective-permute-start | bytes 46088 | tf_op jit(solution)/shard_map/ppermute | solution.py:27
  70.7 21.7 %copy-start.18 = (s32[1024]{0:T(1024)}, s32[1024]{0:T(1024)S(1)}, u32[]{:S(2)}) copy-start(s32[1024]{0:T(1024)S(1)} %pad_clamp_fusion) | copy-start | bytes 12292
  93.3 6.2 %collective-permute-start.6 = (bf16[1,3,64]{2,1,0:T(4,128)(2,1)S(1)}, bf16[1,3,64]{2,1,0:T(4,128)(2,1)S(1)}, u32[]{:S(2)}, u32[]{:S(2)}) collective-permute-start(bf16[1,3,64]{2,1,0:T(4,128)(2,1)S(1)} %get-tuple-element.122), channel_id=1, source_target_pairs={{32,0},{64,32},{96,64},{128,96},{160,128},{192,160},{224,192},{256... | collective-permute-start | bytes 1160 | tf_op jit(solution)/shard_map/ppermute | solution.py:61
  97.3 8.2 %collective-permute-start.7 = (bf16[1,3,64]{2,1,0:T(4,128)(2,1)S(1)}, bf16[1,3,64]{2,1,0:T(4,128)(2,1)S(1)}, u32[]{:S(2)}, u32[]{:S(2)}) collective-permute-start(bf16[1,3,64]{2,1,0:T(4,128)(2,1)S(1)} %get-tuple-element.123), channel_id=1, source_target_pairs={{0,32},{32,64},{64,96},{96,128},{128,160},{160,192},{192,224},{224... | collective-permute-start | bytes 1160 | tf_op jit(solution)/shard_map/ppermute | solution.py:60
  110.5 5.3 %collective-permute-start.8 = (bf16[1,8,64]{2,1,0:T(8,128)(2,1)S(1)}, bf16[1,8,64]{2,1,0:T(8,128)(2,1)S(1)}, u32[]{:S(2)}, u32[]{:S(2)}) collective-permute-start(bf16[1,8,64]{2,1,0:T(8,128)(2,1)S(1)} %get-tuple-element.108), channel_id=1, source_target_pairs={{32,0},{64,32},{96,64},{128,96},{160,128},{192,160},{224,192},{256... | collective-permute-start | bytes 3080 | tf_op jit(solution)/shard_map/ppermute | solution.py:61
  112.5 8.2 %collective-permute-start.9 = (bf16[1,8,64]{2,1,0:T(8,128)(2,1)S(1)}, bf16[1,8,64]{2,1,0:T(8,128)(2,1)S(1)}, u32[]{:S(2)}, u32[]{:S(2)}) collective-permute-start(bf16[1,8,64]{2,1,0:T(8,128)(2,1)S(1)} %get-tuple-element.109), channel_id=1, source_target_pairs={{0,32},{32,64},{64,96},{96,128},{128,160},{160,192},{192,224},{224... | collective-permute-start | bytes 3080 | tf_op jit(solution)/shard_map/ppermute | solution.py:60
  122.5 43.3 %all-to-all-start.1 = ((f32[32,2,30,128]{3,1,2,0:T(2,128)}), f32[32,2,30,128]{3,1,2,0:T(2,128)S(1)}, u32[]{:S(2)}, u32[]{:S(2)}) async-start(f32[32,2,30,128]{3,1,2,0:T(2,128)} %broadcast_in_dim.44), calls=%async_computation.1 | async-start | bytes 1966080 | tf_op jit(solution)/shard_map/all_to_all | solution.py:46
  134.0 31.4 %collective-permute-start.11 = (bf16[2,30,1,128]{3,1,0,2:T(8,128)(2,1)S(1)}, bf16[2,30,1,128]{3,1,0,2:T(8,128)(2,1)S(1)}, u32[]{:S(2)}, u32[]{:S(2)}) collective-permute-start(bf16[2,30,1,128]{3,1,0,2:T(8,128)(2,1)S(1)} %get-tuple-element.75), channel_id=1, source_target_pairs={{0,32},{32,64},{64,96},{96,128},{128,160},{160,192},{192,224},{224... | collective-permute-start | bytes 46088 | tf_op jit(solution)/shard_map/ppermute | solution.py:26
  135.9 29.5 %collective-permute-start.12 = (bf16[2,30,1,128]{3,1,0,2:T(8,128)(2,1)S(1)}, bf16[2,30,1,128]{3,1,0,2:T(8,128)(2,1)S(1)}, u32[]{:S(2)}, u32[]{:S(2)}) collective-permute-start(bf16[2,30,1,128]{3,1,0,2:T(8,128)(2,1)S(1)} %get-tuple-element.76), channel_id=1, source_target_pairs={{32,0},{64,32},{96,64},{128,96},{160,128},{192,160},{224,192},{256... | collective-permute-start | bytes 46088 | tf_op jit(solution)/shard_map/ppermute | solution.py:27
  143.3 19.3 %collective-permute-start.10 = (bf16[2,30,8,1]{3,1,0,2:T(8,128)(2,1)S(1)}, bf16[2,30,8,1]{3,1,0,2:T(8,128)(2,1)S(1)}, u32[]{:S(2)}, u32[]{:S(2)}) collective-permute-start(bf16[2,30,8,1]{3,1,0,2:T(8,128)(2,1)S(1)} %get-tuple-element.77), channel_id=1, source_target_pairs={{0,1},{1,2},{2,3},{3,4},{4,5},{5,6},{6,7},{7,8},{8,9},{9,10},{10,1... | collective-permute-start | bytes 2888 | tf_op jit(solution)/shard_map/ppermute | solution.py:26
  151.4 14.1 %collective-permute-start.13 = (bf16[2,30,8,1]{3,1,0,2:T(8,128)(2,1)S(1)}, bf16[2,30,8,1]{3,1,0,2:T(8,128)(2,1)S(1)}, u32[]{:S(2)}, u32[]{:S(2)}) collective-permute-start(bf16[2,30,8,1]{3,1,0,2:T(8,128)(2,1)S(1)} %get-tuple-element.78), channel_id=1, source_target_pairs={{1,0},{2,1},{3,2},{4,3},{5,4},{6,5},{7,6},{8,7},{9,8},{10,9},{11,1... | collective-permute-start | bytes 2888 | tf_op jit(solution)/shard_map/ppermute | solution.py:27
  179.8 7.1 %collective-permute-start.14 = (bf16[1,3,64]{2,1,0:T(4,128)(2,1)S(1)}, bf16[1,3,64]{2,1,0:T(4,128)(2,1)S(1)}, u32[]{:S(2)}, u32[]{:S(2)}) collective-permute-start(bf16[1,3,64]{2,1,0:T(4,128)(2,1)S(1)} %get-tuple-element.119), channel_id=1, source_target_pairs={{32,0},{64,32},{96,64},{128,96},{160,128},{192,160},{224,192},{256... | collective-permute-start | bytes 1160 | tf_op jit(solution)/shard_map/ppermute | solution.py:61
  181.7 8.5 %collective-permute-start.15 = (bf16[1,3,64]{2,1,0:T(4,128)(2,1)S(1)}, bf16[1,3,64]{2,1,0:T(4,128)(2,1)S(1)}, u32[]{:S(2)}, u32[]{:S(2)}) collective-permute-start(bf16[1,3,64]{2,1,0:T(4,128)(2,1)S(1)} %get-tuple-element.120), channel_id=1, source_target_pairs={{0,32},{32,64},{64,96},{96,128},{128,160},{160,192},{192,224},{224... | collective-permute-start | bytes 1160 | tf_op jit(solution)/shard_map/ppermute | solution.py:60
  (50 other events, 435.2 us)
where the time goes:
time: 192 us; the launch traced here: 191 us
  starting transfers between devices  96.5 us (50%)
  waiting for transfers between devices  41.8 us (22%)
  local copies, waits for them, and re-layouts  32.7 us (17%)
  matrix products  11.8 us (6%)
  other arithmetic  6.35 us (3%)
    all_to_all x2, starting transfers between devices, copy_for_each(): return lax.all_to_all(copies, axis, split_axis=0, concat_axis=0, tiled=True)  30 us
    ppermute x4, waiting for transfers between devices, padded_2(): before = lax.ppermute(last, axis, up)  20.5 us
    ppermute x4, starting transfers between devices, extended(): lax.ppermute(last, axis, up)  19.3 us
    ppermute x4, starting transfers between devices, extended(): lax.ppermute(initial, axis, [(b, a) for a, b in up])  18.4 us
    ppermute x4, starting transfers between devices, padded_2(): after = lax.ppermute(initial, axis, down)  18 us
    ppermute x4, waiting for transfers between devices, extended(): lax.ppermute(last, axis, up)  15.2 us
    ppermute x4, starting transfers between devices, padded_2(): before = lax.ppermute(last, axis, up)  10.7 us
    reshape x2, local copies, waits for them, and re-layouts, joined_along(): tiles.reshape(*dims[:dim], dims[dim] * dims[dim + 1], *dims[dim + 2:])  8.77 us
  transfers between devices with their start and end apart: 18, of which 9 were waited for; matrix products, arithmetic and copies ran while one was open for 2% of the time, Pallas kernels for 0%

commit v1 on v0

v1 whole, which is shorter than its diff:
```python
import math

import jax
import jax.numpy as jnp
from jax import lax
from jax.experimental import pallas as pl
from jax.experimental.pallas import tpu as pltpu
from jax.sharding import PartitionSpec as P

NDIR = 24
NFREQ = 25
LEV = 30
NBAND = 3
STEPS = 2
SLOT = 64
SPEC = NDIR * NFREQ

viscous = 0.2
surface_rate = 0.5
highest = lax.Precision.HIGHEST
MESH = pl.DeviceIdType.MESH
f32 = jnp.float32
bf16 = jnp.bfloat16

KINDS = (
    ("slot", "n"), ("slot", "s"),
    ("key", "n"), ("key", "s"), ("key", "e"), ("key", "w"),
    ("bulk", "n"), ("bulk", "s"), ("bulk", "e"), ("bulk", "w"),
    ("back", "n"), ("back", "s"),
)


def iota(shape, dim):
    return lax.broadcasted_iota(jnp.int32, shape, dim)


def split2(x):
    high = x.astype(bf16)
    low = (x - high.astype(f32)).astype(bf16)
    return high, low


def kernel(
    *refs,
):
    inputs, refs = refs[:22], refs[22:]
    spec_out, vel_out, eta_out, cur_out = refs[:4]
    local, refs = refs[4:26], refs[26:]
    (
        spec_v, wind_ref, cur_ref, wwet_ref, inter_v, rate_ref, gain_ref, stress_ref, stokes_ref,
        vel_v, eta_ref, owet_ref, cor_ref, tau_ref, sprof_ref, thick_ref, mix_ref, fold_ref,
        wsend_ref, orecv_v, osend_ref, wrecv_v,
    ) = local
    (
    wide, energy, transfer, maps16, mall, proj, speed, cos_s, windbuf, curbuf, wwet8,
    whot, ohot, idxbuf, fhot,
    rows_s, tpose, mixp, kmat, coef, orow, fw, vw, kv, forc, keys, backv, forced, smooth,
    sel, ins,
    slot_send, slot_recv, key_send, key_recv, bulk_send, bulk_recv, back_send, back_recv,
    kf_send, kf_all, vwf_send, vwf_all, fold_f,
    ssem, rsem, fs_sem, fr_sem, lsem,
    ) = refs
    n_row, n_col = lax.axis_size("row"), lax.axis_size("col")
    row, col = lax.axis_index("row"), lax.axis_index("col")
    north = (lax.rem(row + 1, n_row), col)
    south = (lax.rem(row + n_row - 1, n_row), col)
    east = (row, lax.rem(col + 1, n_col))
    west = (row, lax.rem(col + n_col - 1, n_col))
    at = {"n": north, "s": south, "e": east, "w": west}
    top = row == n_row - 1
    bottom = row == 0
    barrier = pltpu.get_barrier_semaphore()

    def peer(i):
        return lax.rem(col + i, n_col)

    def signal_to(device):
        pl.semaphore_signal(barrier, inc=1, device_id=device, device_id_type=MESH)

    signal_to(north)
    signal_to(south)

    @pl.when(jnp.logical_not(top))
    def _():
        signal_to(east)
        signal_to(west)

    @pl.when(top)
    def _():
        def tell(i, carry):
            signal_to((row, peer(i)))
            return carry

        lax.fori_loop(1, n_col, tell, 0)

    loads = [pltpu.make_async_copy(src, dst, lsem.at[i]) for i, (src, dst) in enumerate(zip(inputs, local))]
    early = (1, 2, 3, 5, 6, 7, 8, 18)
    for i in early + (0, 4, 10, 11, 12, 13, 14, 15, 16, 17, 20, 9, 19, 21):
        loads[i].start()

    def message(step, kind, way):
        place = step * len(KINDS) + KINDS.index((kind, way))
        index = {"n": 0, "s": 1, "e": 2, "w": 3}[way]
        if kind == "slot":
            src, dst = slot_send.at[step, index], slot_recv.at[step, index]
        elif kind == "key":
            src, dst = key_send.at[step, min(index, 2)], key_recv.at[step, index]
        elif kind == "bulk":
            src, dst = bulk_send.at[step, min(index, 2)], bulk_recv.at[step, index]
        else:
            src, dst = back_send.at[step, index], back_recv.at[step, index]
        return pltpu.make_async_remote_copy(
            src_ref=src, dst_ref=dst, send_sem=ssem.at[place], recv_sem=rsem.at[place],
            device_id=at[way], device_id_type=MESH,
        )

    def fold_copy(step, kind, i):
        src, whole = (kf_send, kf_all) if kind == 0 else (vwf_send, vwf_all)
        place = pl.ds(pl.multiple_of(col * 128, 128), 128)
        return pltpu.make_async_remote_copy(
            src_ref=src.at[step], dst_ref=whole.at[step, :, place],
            send_sem=fs_sem.at[step, kind, i], recv_sem=fr_sem.at[step, kind, col],
            device_id=(row, peer(i)), device_id_type=MESH,
        )

    def fold_wait_recv(step, kind):
        src, whole = (kf_send, kf_all) if kind == 0 else (vwf_send, vwf_all)

        def wait_one(i, carry):
            other = peer(i)
            place = pl.ds(pl.multiple_of(other * 128, 128), 128)
            pltpu.make_async_remote_copy(
                src_ref=src.at[step], dst_ref=whole.at[step, :, place],
                send_sem=fs_sem.at[step, kind, i], recv_sem=fr_sem.at[step, kind, other],
                device_id=(row, other), device_id_type=MESH,
            ).wait_recv()
            return carry

        lax.fori_loop(1, n_col, wait_one, 0)

    def fold_start(step, kind):
        def start_one(i, carry):
            fold_copy(step, kind, i).start()
            return carry

        lax.fori_loop(1, n_col, start_one, 0)

    def fold_wait_send(step, kind):
        def wait_one(i, carry):
            fold_copy(step, kind, i).wait_send()
            return carry

        lax.fori_loop(1, n_col, wait_one, 0)

    for i in early:
        loads[i].wait()
    heading = (iota((NDIR, 128), 0).astype(f32) + 0.5) * (2.0 * math.pi / NDIR)
    cos_s[0] = jnp.cos(heading)
    cos_s[1] = jnp.sin(heading)
    windbuf[...] = jnp.zeros_like(windbuf)
    curbuf[...] = jnp.zeros_like(curbuf)
    for y in range(4):
        lanes = slice(y * 128, (y + 1) * 128)
        for i in range(2):
            windbuf[i : i + 1, lanes] = wind_ref[i, y : y + 1, :]
        for i in range(3):
            curbuf[i : i + 1, lanes] = cur_ref[i, y : y + 1, :]
        wet = jnp.broadcast_to(wwet_ref[y : y + 1, :].astype(f32), (8, 128))
        wwet8[:, lanes] = jnp.where(iota((8, 128), 0) < 2, 1.0, wet)

    def speeds():
        rel_x = windbuf[0:1, :] - curbuf[0:1, :]
        rel_y = windbuf[1:2, :] - curbuf[1:2, :]
        for y in range(4):
            lanes = slice(y * 128, (y + 1) * 128)
            relative = rel_x[:, lanes] * cos_s[0] + rel_y[:, lanes] * cos_s[1]
            speed[:, lanes] = jnp.maximum(relative, 0.0) + jnp.log(1.0 + jnp.exp(-jnp.abs(relative)))

    speeds()

    def one_hot(send_ref, cells):
        idxbuf[...] = jnp.full(idxbuf.shape, -1, jnp.int32)
        for j in range(3):
            idxbuf[0:1, j * 128 : j * 128 + SLOT] = send_ref[j]
        hot = iota((cells, 3 * 128), 0) == idxbuf[0:1, :]
        return jnp.where(hot, 1.0, 0.0).astype(bf16)

    whot[...] = one_hot(wsend_ref, 512)

    maps16[0:2, :] = stress_ref[...]
    maps16[2:8, :] = stokes_ref[...]
    maps16[8:10, :] = stress_ref[...]
    maps16[10:16, :] = stokes_ref[...]
    place = iota((16, SPEC), 1)
    freq = ((place.astype(f32) + 0.5) * (1.0 / NDIR)).astype(jnp.int32)
    direction = place - freq * NDIR
    rate_wide = jnp.zeros((16, SPEC), f32)
    gain_wide = jnp.zeros((16, SPEC), f32)
    for f in range(NFREQ):
        rate_wide = jnp.where(freq == f, rate_ref[0, f], rate_wide)
        gain_wide = jnp.where(freq == f, gain_ref[0, f], gain_wide)
    row16 = iota((16, SPEC), 0)
    half = jnp.where(row16 >= 8, 1, 0)
    maps = maps16[...]
    rated = maps * rate_wide
    for pair in range(12):
        high, low = split2(jnp.where(direction == 2 * pair + half, rated, 0.0))
        mall[pair * 16 : pair * 16 + 16, :] = high
        mall[208 + pair * 16 : 208 + pair * 16 + 16, :] = low

    loads[0].wait()
    wide[...] = spec_v[...].astype(f32)
    for y in range(4):
        energy[0, :, y * 128 : (y + 1) * 128] = wide[pl.ds(y, SPEC, stride=4), :].astype(bf16)

    loads[4].wait()
    inter = inter_v[...]
    first = maps.astype(bf16)
    rest = maps - first.astype(f32)
    second = rest.astype(bf16)
    third = (rest - second.astype(f32)).astype(bf16)
    moved = (
        jnp.dot(first, inter, preferred_element_type=f32)
        + jnp.dot(second, inter, preferred_element_type=f32)
        + jnp.dot(third, inter, preferred_element_type=f32)
    )
    last_pair = jnp.where(row16 < 8, maps + moved, maps * gain_wide)
    last_pair = jnp.where((row16 < 2) | ((row16 >= 8) & (row16 < 10)), 0.0, last_pair)
    high, low = split2(last_pair)
    mall[192:208, :] = high
    mall[400:416, :] = low

    def project(step):
        both = jnp.dot(mall[...], energy[step], preferred_element_type=f32)
        proj[...] = both[0:208] + both[208:416]

    def send_slots(step):
        total = proj[192:200, :] + curbuf[2:3, :] * proj[200:208, :]
        for k in range(NDIR):
            total = total + speed[k : k + 1, :] * proj[8 * k : 8 * k + 8, :]
        fields = (total * wwet8[...]).astype(bf16)
        slots = jnp.dot(fields, whot[...], preferred_element_type=f32)
        slot_send[step, 1] = slots[:, 0:128]
        slot_send[step, 0] = slots[:, 256:384]
        return slots[:, 128 : 128 + SLOT].astype(bf16)

    project(0)
    own_slots = send_slots(0)

    @pl.when(jnp.logical_not(top))
    def _():
        pl.semaphore_wait(barrier, 4)

    @pl.when(top)
    def _():
        pl.semaphore_wait(barrier, n_col + 1)

    def start(step, kind):
        sent = [message(step, kind, way) for k, way in KINDS if k == kind]
        for copy in sent:
            copy.start()
        return sent

    pending = []
    slot_msgs = start(0, "slot")
    pending += slot_msgs

    for i in (10, 11, 12, 13, 14, 15, 16, 17, 20):
        loads[i].wait()
    for y in range(8):
        lanes = slice(y * 128, (y + 1) * 128)
        wet = owet_ref[y : y + 1, :].astype(f32)
        orow[0:1, lanes] = wet
        wet8 = jnp.broadcast_to(wet, (8, 128))
        cor8 = jnp.broadcast_to(cor_ref[y : y + 1, :], (8, 128))
        fw[:, lanes] = jnp.where(iota((8, 128), 0) < 2, wet8, wet8 * cor8)
        backv[:, lanes] = jnp.broadcast_to(eta_ref[y : y + 1, :], (8, 128))
    rows_s[...] = jnp.zeros_like(rows_s)
    rows_s[0:1, 0:LEV] = mix_ref[0:1, :]
    rows_s[1:2, 0:LEV] = tau_ref[...]
    rows_s[2:5, 0:LEV] = sprof_ref[...]
    rows_s[5:6, 0:LEV] = thick_ref[...]
    mixp[...] = jnp.zeros_like(mixp)
    mixp[0:LEV, 0:LEV] = mix_ref[...]

    def wide_row(i):
        return jnp.broadcast_to(rows_s[i : i + 1, :], (8, 128))

    r8 = iota((8, 128), 0)
    lane8 = iota((8, 128), 1)
    along_u = jnp.where(r8 == 0, wide_row(1), 0.0)
    along_v = jnp.where(r8 == 1, wide_row(1), 0.0)
    for b in range(NBAND):
        along_u = jnp.where(r8 == 3 + 2 * b, wide_row(2 + b), along_u)
        along_v = jnp.where(r8 == 2 + 2 * b, -wide_row(2 + b), along_v)
    tpose[...] = jnp.zeros_like(tpose)
    tpose[0:8, :] = along_u
    tpose[8:16, :] = along_v
    turned = jnp.transpose(tpose[...])
    gain_u = turned[0:32, 0:8]
    gain_v = turned[0:32, 8:16]
    m0, thick = wide_row(0), wide_row(5)
    for i, (profile, weight) in enumerate(((along_u, m0), (along_v, m0), (along_u, thick), (along_v, thick))):
        coef[i] = jnp.broadcast_to(jnp.sum(profile * weight, axis=1, keepdims=True), (8, 128))
    m0_far = pltpu.roll(m0, 32, 1)
    thick_far = pltpu.roll(thick, 32, 1)
    kmat[...] = jnp.where(
        r8 == 0, m0, jnp.where(r8 == 1, m0_far, jnp.where(r8 == 2, thick, jnp.where(r8 == 3, thick_far, 0.0)))
    )

    cell = iota((1024, 128), 0)
    spot = iota((1024, 128), 1)
    edge = jnp.where(spot < 8, spot * 128 + 127, jnp.where(spot < 16, (spot - 8) * 128, -1))
    sel[...] = jnp.where(cell == edge, 1.0, 0.0).astype(bf16)
    cell_t = iota((128, 1024), 1)
    spot_t = iota((128, 1024), 0)
    edge_t = jnp.where(spot_t < 8, spot_t * 128, jnp.where(spot_t < 16, (spot_t - 8) * 128 + 127, -1))
    ins[...] = jnp.where(cell_t == edge_t, 1.0, 0.0).astype(bf16)

    ohot[...] = one_hot(osend_ref, 1024)

    @pl.when(top)
    def _():
        hot = iota((n_col * 128, 128), 0) == fold_ref[...]
        fhot[...] = jnp.where(hot, 1.0, 0.0).astype(bf16)

    def prepare_ocean(step):
        kv[...] = jnp.dot(kmat[:, 0:64], vw[...], precision=highest, preferred_element_type=f32)

        @pl.when(top)
        def _():
            line = vw[:, 7 * 128 : 8 * 128].astype(bf16)
            vwf_send[step] = line
            vwf_all[step, :, pl.ds(pl.multiple_of(col * 128, 128), 128)] = line
            fold_start(step, 1)

    loads[9].wait()
    vw[...] = jnp.zeros_like(vw)
    for c in range(2):
        for y in range(8):
            lanes = slice(y * 128, (y + 1) * 128)
            level = vel_v[pl.ds(c * 8 * LEV + y, LEV, stride=8), :]
            vw[c * 32 : c * 32 + LEV, lanes] = level * orow[0:1, lanes]
    prepare_ocean(0)

    def next_transfer(step):
        transfer[...] = jnp.dot(inter_v[...], energy[step], preferred_element_type=f32)

    def update_energy(step):
        level = curbuf[2:3, :]
        wet = wwet8[2:3, :]
        for pair in range(13):
            count = 2 if pair < 12 else 1
            rows = slice(pair * 48, pair * 48 + 24 * count)
            old = energy[step, rows, :].astype(f32)
            parts = []
            for part in range(count):
                f = 2 * pair + part
                e = old[part * 24 : part * 24 + 24]
                t = transfer[f * 24 : f * 24 + 24, :]
                factor = rate_ref[0, f] * speed[...] + gain_ref[0, f] * level
                parts.append(wet * (e + factor * e + t))
            new = parts[0] if count == 1 else jnp.concatenate(parts, axis=0)
            if step == STEPS - 1:
                base, size = pair * 192, 96 * count
                for y in range(4):
                    wide[pl.ds(base + y, 24 * count, stride=4), :] = new[:, y * 128 : (y + 1) * 128]
                spec_out[base : base + size, :] = wide[base : base + size, :].astype(bf16)
            else:
                energy[step + 1, rows, :] = new.astype(bf16)

    next_transfer(0)
    update_energy(0)
    loads[19].wait()
    loads[21].wait()

    def pass_north(step, own_slots, slot_msgs):
        for copy in slot_msgs:
            copy.wait_recv()
        from_south = jnp.where(bottom, 0.0, slot_recv[step, 0][:, 0:SLOT]).astype(bf16)
        from_north = jnp.where(top, 0.0, slot_recv[step, 1][:, 0:SLOT]).astype(bf16)
        force = (
            jnp.dot(from_north, orecv_v[0:64, :], preferred_element_type=f32)
            + jnp.dot(own_slots, orecv_v[64:128, :], preferred_element_type=f32)
            + jnp.dot(from_south, orecv_v[128:192, :], preferred_element_type=f32)
        )
        force = force * fw[...]
        forc[...] = force
        for y in range(8):
            lanes = slice(y * 128, (y + 1) * 128)
            tile = force[:, lanes]
            value = kv[:, lanes]
            for i in range(4):
                extra = jnp.sum(tile * coef[i], axis=0, keepdims=True)
                value = value + jnp.where(r8 == i, extra, 0.0)
            keys[y] = value
        key_send[step, 0] = keys[7]
        key_send[step, 1] = keys[0]
        edges = jnp.zeros((8, 128), f32)
        for y in range(8):
            edges = jnp.where(lane8 == y, pltpu.roll(keys[y], y + 1, 1), edges)
            edges = jnp.where(lane8 == 8 + y, pltpu.roll(keys[y], 8 + y, 1), edges)
        key_send[step, 2] = edges
        msgs = start(step, "key")

        @pl.when(top)
        def _():
            line = jnp.concatenate([keys[7], forc[:, 7 * 128 : 8 * 128]], axis=0).astype(bf16)
            kf_send[step] = line
            kf_all[step, :, pl.ds(pl.multiple_of(col * 128, 128), 128)] = line
            fold_start(step, 0)

        force = forc[...]
        for c, gain in enumerate((gain_u, gain_v)):
            forced[c * 32 : c * 32 + 32, :] = vw[c * 32 : c * 32 + 32, :] + jnp.dot(
                gain, force, precision=highest, preferred_element_type=f32
            )
        low = forced[...].astype(bf16)
        bulk_send[step, 0] = low[:, 7 * 128 : 8 * 128]
        bulk_send[step, 1] = low[:, 0:128]
        bulk_send[step, 2] = jnp.dot(low, sel[...], preferred_element_type=f32).astype(bf16)
        bulks = start(step, "bulk")
        return msgs, bulks

    def finish_keys(step, msgs):
        for copy in msgs:
            copy.wait_recv()

        @pl.when(top)
        def _():
            fold_wait_recv(step, 0)
            chosen = jnp.dot(kf_all[step], fhot[...], preferred_element_type=f32)
            key_recv[step, 1] = -chosen[0:8]
            fold_f[...] = chosen[8:16]

        south_halo = jnp.where(bottom, 0.0, key_recv[step, 0])
        north_halo = key_recv[step, 1]
        from_west = key_recv[step, 2]
        from_east = key_recv[step, 3]
        backs = []
        for y in range(8):
            lanes = slice(y * 128, (y + 1) * 128)
            here = keys[y]
            up = keys[y + 1] if y < 7 else north_halo
            down = keys[y - 1] if y > 0 else south_halo
            left_in = from_west if y == 0 else pltpu.roll(from_west, 128 - y, 1)
            right_in = pltpu.roll(from_east, 127 - (8 + y), 1)
            left = jnp.where(lane8 == 0, left_in, pltpu.roll(here, 1, 1))
            right = jnp.where(lane8 == 127, right_in, pltpu.roll(here, 127, 1))
            wet = jnp.broadcast_to(orow[0:1, lanes], (8, 128))
            level = here + viscous * (up + down + left + right - 4.0 * here)
            spread = 0.5 * (right - left) + 0.5 * pltpu.roll(up - down, 7, 0)
            elevation = backv[:, lanes] - surface_rate * spread
            value = wet * jnp.where(r8 < 2, level, jnp.where(r8 == 2, elevation, 0.0))
            backv[:, lanes] = value
            if step == STEPS - 1:
                eta_out[y : y + 1, :] = value[2:3, :]
        slots = jnp.dot(backv[...].astype(bf16), ohot[...], preferred_element_type=f32)
        back_send[step, 1] = slots[:, 0:128]
        back_send[step, 0] = slots[:, 256:384]
        own = slots[:, 128 : 128 + SLOT].astype(bf16)
        return own, start(step, "back")

    def finish_current(step, own, msgs):
        for copy in msgs:
            copy.wait_recv()
        from_south = jnp.where(bottom, 0.0, back_recv[step, 0][:, 0:SLOT]).astype(bf16)
        from_north = jnp.where(top, 0.0, back_recv[step, 1][:, 0:SLOT]).astype(bf16)
        curbuf[...] = (
            jnp.dot(from_north, wrecv_v[0:64, :], preferred_element_type=f32)
            + jnp.dot(own, wrecv_v[64:128, :], preferred_element_type=f32)
            + jnp.dot(from_south, wrecv_v[128:192, :], preferred_element_type=f32)
        )

    def finish_velocity(step, bulks):
        for copy in bulks:
            copy.wait_recv()

        @pl.when(top)
        def _():
            fold_wait_recv(step, 1)
            chosen = jnp.dot(vwf_all[step], fhot[...], preferred_element_type=f32)
            added = jnp.concatenate(
                [
                    jnp.dot(gain, fold_f[...], precision=highest, preferred_element_type=f32)
                    for gain in (gain_u, gain_v)
                ],
                axis=0,
            )
            bulk_recv[step, 1] = (-(chosen + added)).astype(bf16)

        south_halo = jnp.where(bottom, 0.0, bulk_recv[step, 0].astype(f32))
        north_halo = bulk_recv[step, 1].astype(f32)
        lane64 = iota((64, 128), 1)
        sides = jnp.where(lane64 < 8, bulk_recv[step, 2].astype(f32), bulk_recv[step, 3].astype(f32))
        outer = jnp.dot(sides.astype(bf16), ins[...], preferred_element_type=f32)
        for y in range(8):
            lanes = slice(y * 128, (y + 1) * 128)
            here = forced[:, lanes]
            up = forced[:, (y + 1) * 128 : (y + 2) * 128] if y < 7 else north_halo
            down = forced[:, (y - 1) * 128 : y * 128] if y > 0 else south_halo
            left = jnp.where(lane64 == 0, 0.0, pltpu.roll(here, 1, 1))
            right = jnp.where(lane64 == 127, 0.0, pltpu.roll(here, 127, 1))
            around = up + down + left + right + outer[:, lanes] - 4.0 * here
            smooth[:, lanes] = orow[0:1, lanes] * (here + viscous * around)
        for c in range(2):
            new = jnp.dot(
                mixp[...], smooth[c * 32 : c * 32 + 32, :], precision=highest, preferred_element_type=f32
            )
            if step == STEPS - 1:
                for y in range(8):
                    vel_out[pl.ds(c * 8 * LEV + y, LEV, stride=8), :] = new[0:LEV, y * 128 : (y + 1) * 128]
            else:
                vw[c * 32 : c * 32 + 32, :] = new * orow[0:1, :]

    for step in range(STEPS):
        keys_sent, bulks = pass_north(step, own_slots, slot_msgs)
        pending += keys_sent + bulks
        if step == 0:
            project(1)
        else:
            update_energy(step)
        own_back, backs = finish_keys(step, keys_sent)
        pending += backs
        if step == 0:
            next_transfer(1)
        else:
            finish_velocity(step, bulks)
        finish_current(step, own_back, backs)
        if step == 0:
            speeds()
            own_slots = send_slots(1)
            slot_msgs = start(1, "slot")
            pending += slot_msgs
            finish_velocity(step, bulks)
            prepare_ocean(1)
    for y in range(4):
        for i in range(3):
            cur_out[i, y : y + 1, :] = curbuf[i : i + 1, y * 128 : (y + 1) * 128]
    for copy in pending:
        copy.wait_send()

    @pl.when(top)
    def _():
        for step in range(STEPS):
            for kind in range(2):
                fold_wait_send(step, kind)


def shards(
    spectra, wind, wave_current, wave_wet, interaction, input_rate, eta_gain, stress_map, stokes_map,
    ocean_vel, ocean_eta, ocean_wet, coriolis, tau_profile, stokes_profile, thickness, mix_inverse,
    fold_index, wave_send, ocean_recv, ocean_send, wave_recv,
):
    n_col = lax.axis_size("col")
    vmem = pl.BlockSpec(memory_space=pltpu.VMEM)
    hbm = pl.BlockSpec(memory_space=pltpu.HBM)
    V = pltpu.VMEM
    scratch = [
        V((2400, 128), f32), V((STEPS, SPEC, 512), bf16), V((SPEC, 512), f32), V((16, SPEC), f32),
        V((416, SPEC), bf16), V((208, 512), f32), V((NDIR, 512), f32), V((2, NDIR, 128), f32),
        V((8, 512), f32), V((8, 512), f32), V((8, 512), f32),
        V((512, 384), bf16), V((1024, 384), bf16), V((1, 384), jnp.int32), V((n_col * 128, 128), bf16),
        V((8, 128), f32), V((128, 128), f32), V((32, 32), f32), V((8, 128), f32), V((4, 8, 128), f32),
        V((1, 1024), f32), V((8, 1024), f32), V((64, 1024), f32), V((8, 1024), f32), V((8, 1024), f32),
        V((8, 8, 128), f32), V((8, 1024), f32), V((64, 1024), f32), V((64, 1024), f32),
        V((1024, 128), bf16), V((128, 1024), bf16),
        V((STEPS, 2, 8, 128), f32), V((STEPS, 2, 8, 128), f32),
        V((STEPS, 3, 8, 128), f32), V((STEPS, 4, 8, 128), f32),
        V((STEPS, 3, 64, 128), bf16), V((STEPS, 4, 64, 128), bf16),
        V((STEPS, 2, 8, 128), f32), V((STEPS, 2, 8, 128), f32),
        V((STEPS, 16, 128), bf16), V((STEPS, 16, n_col * 128), bf16),
        V((STEPS, 64, 128), bf16), V((STEPS, 64, n_col * 128), bf16), V((8, 128), f32),
        pltpu.SemaphoreType.DMA((STEPS * len(KINDS),)), pltpu.SemaphoreType.DMA((STEPS * len(KINDS),)),
        pltpu.SemaphoreType.DMA((STEPS, 2, n_col)), pltpu.SemaphoreType.DMA((STEPS, 2, n_col)),
        pltpu.SemaphoreType.DMA((22,)),
    ]
    operands = (
        spectra.reshape(2400, 128), wind, wave_current, wave_wet, interaction,
        input_rate.reshape(1, NFREQ), eta_gain.reshape(1, NFREQ), stress_map, stokes_map,
        ocean_vel.reshape(480, 128), ocean_eta, ocean_wet, coriolis,
        tau_profile.reshape(1, LEV), stokes_profile, thickness.reshape(1, LEV), mix_inverse,
        fold_index.reshape(1, 128),
        wave_send.reshape(3, 1, SLOT), ocean_recv.reshape(192, 1024),
        ocean_send.reshape(3, 1, SLOT), wave_recv.reshape(192, 512),
    )
    held = [(pltpu.SMEM if i in (5, 6) else V)(x.shape, x.dtype) for i, x in enumerate(operands)]
    spec_out, vel_out, eta_out, cur_out = pl.pallas_call(
        kernel,
        name="coupled",
        out_shape=(
            jax.ShapeDtypeStruct((2400, 128), bf16),
            jax.ShapeDtypeStruct((480, 128), f32),
            jax.ShapeDtypeStruct((8, 128), f32),
            jax.ShapeDtypeStruct((3, 4, 128), f32),
        ),
        in_specs=[hbm] * len(operands),
        out_specs=(vmem, vmem, vmem, vmem),
        scratch_shapes=held + scratch,
        compiler_params=pltpu.CompilerParams(
            collective_id=0, has_side_effects=True, vmem_limit_bytes=40 * 1024 * 1024
        ),
    )(*[pltpu.with_memory_space_constraint(x, pltpu.HBM) for x in operands])
    return (
        spec_out.reshape(SPEC, 4, 128),
        vel_out.reshape(2, LEV, 8, 128),
        eta_out,
        cur_out,
    )


def solution(mesh):
    tiled3 = P(None, "row", "col")
    tiled = P("row", "col")
    in_specs = (
        tiled3, tiled3, tiled3, tiled, P(), P(), P(), P(), P(),
        P(None, None, "row", "col"), tiled, tiled, tiled, P(), P(), P(), P(), P("col"),
        P("row", "col", None, None), P("row", "col", None, None, None),
        P("row", "col", None, None), P("row", "col", None, None, None),
    )
    out_specs = (tiled3, P(None, None, "row", "col"), tiled, tiled3)
    return jax.shard_map(shards, mesh=mesh, in_specs=in_specs, out_specs=out_specs, check_vma=False)
```

time: 192 us -> 81.6 us (0.42)
  the two profiles are of different devices: /device:TPU:65 before, /device:TPU:1 now
where the time goes in v1:
time: 81.6 us; the launch traced here: 81.4 us
  Pallas kernels  78.1 us (96%)
  local copies, waits for them, and re-layouts  2.7 us (3%)
    pallas_call x1, Pallas kernels, shards(): pl.pallas_call(kernel, name='coupled', out_shape=(jax.ShapeDtypeStruct((2...  78.1 us
    unnamed x4, local copies, waits for them, and re-layouts  2.7 us

profile of v1, /device:TPU:1, one launch (start us, length us, event | category | flops | bytes accessed | tf_op | source)
XLA Modules:
  0.0 81.4 jit_solution(13738473450631289169)
XLA Ops:
  0.6 78.1 %coupled.1 = (bf16[2400,128]{1,0:T(8,128)(2,1)S(1)}, f32[480,128]{1,0:T(8,128)S(1)}, f32[8,128]{1,0:T(8,128)S(1)}, f32[3,4,128]{2,1,0:T(4,128)S(1)}) custom-call(bf16[2400,128]{1,0:T(8,128)(2,1)} %bitcast.15, f32[2,4,128]{2,1,0:T(4,128)} %refs_1_.1, f32[3,4,128]{2,1,0:T(4,128)} %refs_2_.1, s32[4,128]{1,0:T(4,128)} %refs_3_.1, bf16[600,600]{1,0:T(8,128)(2,1)} %refs_4_.1, ...), custom_call_target="tpu_custom_call" | custom-call | tf_op jit(solution)/shard_map/coupled/pallas_call | solution.py:588
  78.7 0.8 %copy.30 = bf16[600,4,128]{2,1,0:T(4,128)(2,1)} copy(bf16[600,4,128]{2,1,0:T(4,128)(2,1)S(1)} %bitcast.13) | data formatting | bytes 1228800
  79.6 0.7 copy.31
  80.2 0.6 copy.32
  80.8 0.6 copy.33

commit v2 on v1

--- a/solution.py
+++ b/solution.py
@@ -14,6 +14,7 @@
 STEPS = 2
 SLOT = 64
 SPEC = NDIR * NFREQ
+GROUP = 4
 
 viscous = 0.2
 surface_rate = 0.5
@@ -57,8 +58,8 @@
     rows_s, tpose, mixp, kmat, coef, orow, fw, vw, kv, forc, keys, backv, forced, smooth,
     sel, ins,
     slot_send, slot_recv, key_send, key_recv, bulk_send, bulk_recv, back_send, back_recv,
-    kf_send, kf_all, vwf_send, vwf_all, fold_f,
-    ssem, rsem, fs_sem, fr_sem, lsem,
+    kf_send, kf_all, line_send, lines, chosen_send, chosen_all, index_send, index_all, lhot,
+    ssem, rsem, fs_sem, fr_sem, far_s, far_r, near_s, near_r, index_s, index_r, lsem,
     ) = refs
     n_row, n_col = lax.axis_size("row"), lax.axis_size("col")
     row, col = lax.axis_index("row"), lax.axis_index("col")
@@ -77,11 +78,13 @@
     def signal_to(device):
         pl.semaphore_signal(barrier, inc=1, device_id=device, device_id_type=MESH)
 
-    signal_to(north)
-    signal_to(south)
+    @pl.when(jnp.logical_not(bottom))
+    def _():
+        signal_to(south)
 
     @pl.when(jnp.logical_not(top))
     def _():
+        signal_to(north)
         signal_to(east)
         signal_to(west)
 
@@ -114,43 +117,51 @@
             device_id=at[way], device_id_type=MESH,
         )
 
-    def fold_copy(step, kind, i):
-        src, whole = (kf_send, kf_all) if kind == 0 else (vwf_send, vwf_all)
-        place = pl.ds(pl.multiple_of(col * 128, 128), 128)
+    n_far = n_col // GROUP
+    far_block = col // GROUP
+    member = lax.rem(col, GROUP)
+
+    def lanes_of(i):
+        return pl.ds(pl.multiple_of(i * 128, 128), 128)
+
+    def key_copy(step, i, sender):
         return pltpu.make_async_remote_copy(
-            src_ref=src.at[step], dst_ref=whole.at[step, :, place],
-            send_sem=fs_sem.at[step, kind, i], recv_sem=fr_sem.at[step, kind, col],
+            src_ref=kf_send.at[step], dst_ref=kf_all.at[step, :, lanes_of(sender)],
+            send_sem=fs_sem.at[step, i], recv_sem=fr_sem.at[step, sender],
             device_id=(row, peer(i)), device_id_type=MESH,
         )
 
-    def fold_wait_recv(step, kind):
-        src, whole = (kf_send, kf_all) if kind == 0 else (vwf_send, vwf_all)
-
-        def wait_one(i, carry):
-            other = peer(i)
-            place = pl.ds(pl.multiple_of(other * 128, 128), 128)
-            pltpu.make_async_remote_copy(
-                src_ref=src.at[step], dst_ref=whole.at[step, :, place],
-                send_sem=fs_sem.at[step, kind, i], recv_sem=fr_sem.at[step, kind, other],
-                device_id=(row, other), device_id_type=MESH,
-            ).wait_recv()
+    def key_fold(step, act, receiving=False):
+        def one(i, carry):
+            act(key_copy(step, i, peer(i) if receiving else col))
             return carry
 
-        lax.fori_loop(1, n_col, wait_one, 0)
-
-    def fold_start(step, kind):
-        def start_one(i, carry):
-            fold_copy(step, kind, i).start()
-            return carry
-
-        lax.fori_loop(1, n_col, start_one, 0)
-
-    def fold_wait_send(step, kind):
-        def wait_one(i, carry):
-            fold_copy(step, kind, i).wait_send()
-            return carry
-
-        lax.fori_loop(1, n_col, wait_one, 0)
+        lax.fori_loop(1, n_col, one, 0)
+
+    def far_copy(step, i, sender):
+        return pltpu.make_async_remote_copy(
+            src_ref=line_send.at[step], dst_ref=lines.at[step, :, lanes_of(sender)],
+            send_sem=far_s.at[step, i], recv_sem=far_r.at[step, sender],
+            device_id=(row, peer(i * GROUP)), device_id_type=MESH,
+        )
+
+    def near_copy(step, i, sender):
+        other = far_block * GROUP + lax.rem(member + i, GROUP)
+        return pltpu.make_async_remote_copy(
+            src_ref=chosen_send.at[step, i], dst_ref=chosen_all.at[step, sender],
+            send_sem=near_s.at[step, i], recv_sem=near_r.at[step, sender],
+            device_id=(row, other), device_id_type=MESH,
+        )
+
+    near_part = member
+
+    def index_copy(i, sender):
+        other = far_block * GROUP + lax.rem(member + i, GROUP)
+        return pltpu.make_async_remote_copy(
+            src_ref=index_send, dst_ref=index_all.at[sender],
+            send_sem=index_s.at[i], recv_sem=index_r.at[sender],
+            device_id=(row, other), device_id_type=MESH,
+        )
 
     for i in early:
         loads[i].wait()
@@ -247,25 +258,51 @@
     project(0)
     own_slots = send_slots(0)
 
-    @pl.when(jnp.logical_not(top))
+    @pl.when(jnp.logical_not(top | bottom))
     def _():
         pl.semaphore_wait(barrier, 4)
 
+    @pl.when(bottom)
+    def _():
+        pl.semaphore_wait(barrier, 3)
+
     @pl.when(top)
     def _():
-        pl.semaphore_wait(barrier, n_col + 1)
+        pl.semaphore_wait(barrier, n_col)
+
+    def each(msgs, act, receiving):
+        for way, copy in msgs:
+            edge = {"n": bottom if receiving else top, "s": top if receiving else bottom}.get(way)
+            if edge is None:
+                act(copy)
+            else:
+                pl.when(jnp.logical_not(edge))(lambda copy=copy: act(copy))
 
     def start(step, kind):
-        sent = [message(step, kind, way) for k, way in KINDS if k == kind]
-        for copy in sent:
-            copy.start()
+        sent = [(way, message(step, kind, way)) for k, way in KINDS if k == kind]
+        each(sent, lambda copy: copy.start(), False)
         return sent
+
+    def wait_for(msgs):
+        each(msgs, lambda copy: copy.wait_recv(), True)
 
     pending = []
     slot_msgs = start(0, "slot")
     pending += slot_msgs
 
-    for i in (10, 11, 12, 13, 14, 15, 16, 17, 20):
+    @pl.when(top)
+    def _():
+        loads[17].wait()
+        index_send[...] = jnp.broadcast_to(fold_ref[...].astype(f32), (8, 128))
+        index_all[member] = index_send[...]
+        for i in range(1, GROUP):
+            index_copy(i, member).start()
+
+    @pl.when(jnp.logical_not(top))
+    def _():
+        loads[17].wait()
+
+    for i in (10, 11, 12, 13, 14, 15, 16, 20):
         loads[i].wait()
     for y in range(8):
         lanes = slice(y * 128, (y + 1) * 128)
@@ -326,13 +363,6 @@
 
     def prepare_ocean(step):
         kv[...] = jnp.dot(kmat[:, 0:64], vw[...], precision=highest, preferred_element_type=f32)
-
-        @pl.when(top)
-        def _():
-            line = vw[:, 7 * 128 : 8 * 128].astype(bf16)
-            vwf_send[step] = line
-            vwf_all[step, :, pl.ds(pl.multiple_of(col * 128, 128), 128)] = line
-            fold_start(step, 1)
 
     loads[9].wait()
     vw[...] = jnp.zeros_like(vw)
@@ -375,8 +405,7 @@
     loads[21].wait()
 
     def pass_north(step, own_slots, slot_msgs):
-        for copy in slot_msgs:
-            copy.wait_recv()
+        wait_for(slot_msgs)
         from_south = jnp.where(bottom, 0.0, slot_recv[step, 0][:, 0:SLOT]).astype(bf16)
         from_north = jnp.where(top, 0.0, slot_recv[step, 1][:, 0:SLOT]).astype(bf16)
         force = (
@@ -405,10 +434,10 @@
 
         @pl.when(top)
         def _():
-            line = jnp.concatenate([keys[7], forc[:, 7 * 128 : 8 * 128]], axis=0).astype(bf16)
+            line = keys[7].astype(bf16)
             kf_send[step] = line
-            kf_all[step, :, pl.ds(pl.multiple_of(col * 128, 128), 128)] = line
-            fold_start(step, 0)
+            kf_all[step, :, lanes_of(col)] = line
+            key_fold(step, lambda copy: copy.start())
 
         force = forc[...]
         for c, gain in enumerate((gain_u, gain_v)):
@@ -420,18 +449,45 @@
         bulk_send[step, 1] = low[:, 0:128]
         bulk_send[step, 2] = jnp.dot(low, sel[...], preferred_element_type=f32).astype(bf16)
         bulks = start(step, "bulk")
-        return msgs, bulks
-
-    def finish_keys(step, msgs):
-        for copy in msgs:
-            copy.wait_recv()
 
         @pl.when(top)
         def _():
-            fold_wait_recv(step, 0)
-            chosen = jnp.dot(kf_all[step], fhot[...], preferred_element_type=f32)
-            key_recv[step, 1] = -chosen[0:8]
-            fold_f[...] = chosen[8:16]
+            line = low[:, 7 * 128 : 8 * 128]
+            line_send[step] = line
+            lines[step, :, lanes_of(far_block)] = line
+            for i in range(1, n_far):
+                far_copy(step, i, far_block).start()
+
+        return msgs, bulks
+
+    def select_lines(step):
+        @pl.when(top)
+        def _():
+            if step == 0:
+                for i in range(1, GROUP):
+                    index_copy(i, lax.rem(member + i, GROUP)).wait_recv()
+                spot = iota((n_far * 128, 128), 0)
+                column = (spot // 128) * (GROUP * 128) + lax.rem(spot, 128) + member * 128
+                for i in range(GROUP):
+                    wanted = index_all[lax.rem(member + i, GROUP)][0:1, :].astype(jnp.int32)
+                    lhot[i] = jnp.where(column == wanted, 1.0, 0.0).astype(bf16)
+            for i in range(1, n_far):
+                far_copy(step, i, lax.rem(far_block + i, n_far)).wait_recv()
+            for i in range(GROUP):
+                chosen = jnp.dot(lines[step], lhot[i], preferred_element_type=f32).astype(bf16)
+                if i == 0:
+                    chosen_all[step, member] = chosen
+                else:
+                    chosen_send[step, i] = chosen
+                    near_copy(step, i, near_part).start()
+
+    def finish_keys(step, msgs):
+        wait_for(msgs)
+
+        @pl.when(top)
+        def _():
+            key_fold(step, lambda copy: copy.wait_recv(), True)
+            key_recv[step, 1] = -jnp.dot(kf_all[step], fhot[...], preferred_element_type=f32)
 
         south_halo = jnp.where(bottom, 0.0, key_recv[step, 0])
         north_halo = key_recv[step, 1]
@@ -462,8 +518,7 @@
         return own, start(step, "back")
 
     def finish_current(step, own, msgs):
-        for copy in msgs:
-            copy.wait_recv()
+        wait_for(msgs)
         from_south = jnp.where(bottom, 0.0, back_recv[step, 0][:, 0:SLOT]).astype(bf16)
         from_north = jnp.where(top, 0.0, back_recv[step, 1][:, 0:SLOT]).astype(bf16)
         curbuf[...] = (
@@ -473,21 +528,16 @@
         )
 
     def finish_velocity(step, bulks):
-        for copy in bulks:
-            copy.wait_recv()
+        wait_for(bulks)
 
         @pl.when(top)
         def _():
-            fold_wait_recv(step, 1)
-            chosen = jnp.dot(vwf_all[step], fhot[...], preferred_element_type=f32)
-            added = jnp.concatenate(
-                [
-                    jnp.dot(gain, fold_f[...], precision=highest, preferred_element_type=f32)
-                    for gain in (gain_u, gain_v)
-                ],
-                axis=0,
-            )
-            bulk_recv[step, 1] = (-(chosen + added)).astype(bf16)
+            for i in range(1, GROUP):
+                near_copy(step, i, lax.rem(member + i, GROUP)).wait_recv()
+            total = chosen_all[step, 0].astype(f32)
+            for i in range(1, GROUP):
+                total = total + chosen_all[step, i].astype(f32)
+            bulk_recv[step, 1] = (-total).astype(bf16)
 
         south_halo = jnp.where(bottom, 0.0, bulk_recv[step, 0].astype(f32))
         north_halo = bulk_recv[step, 1].astype(f32)
@@ -522,10 +572,11 @@
             update_energy(step)
         own_back, backs = finish_keys(step, keys_sent)
         pending += backs
+        select_lines(step)
         if step == 0:
             next_transfer(1)
         else:
-            finish_velocity(step, bulks)
+            pl.when(jnp.logical_not(top))(lambda: finish_velocity(step, bulks))
         finish_current(step, own_back, backs)
         if step == 0:
             speeds()
@@ -537,14 +588,19 @@
     for y in range(4):
         for i in range(3):
             cur_out[i, y : y + 1, :] = curbuf[i : i + 1, y * 128 : (y + 1) * 128]
-    for copy in pending:
-        copy.wait_send()
+    pl.when(top)(lambda: finish_velocity(STEPS - 1, bulks))
+    each(pending, lambda copy: copy.wait_send(), False)
 
     @pl.when(top)
     def _():
         for step in range(STEPS):
-            for kind in range(2):
-                fold_wait_send(step, kind)
+            key_fold(step, lambda copy: copy.wait_send())
+            for i in range(1, n_far):
+                far_copy(step, i, far_block).wait_send()
+            for i in range(1, GROUP):
+                near_copy(step, i, near_part).wait_send()
+        for i in range(1, GROUP):
+            index_copy(i, member).wait_send()
 
 
 def shards(
@@ -553,6 +609,7 @@
     fold_index, wave_send, ocean_recv, ocean_send, wave_recv,
 ):
     n_col = lax.axis_size("col")
+    n_far = n_col // GROUP
     vmem = pl.BlockSpec(memory_space=pltpu.VMEM)
     hbm = pl.BlockSpec(memory_space=pltpu.HBM)
     V = pltpu.VMEM
@@ -569,10 +626,15 @@
         V((STEPS, 3, 8, 128), f32), V((STEPS, 4, 8, 128), f32),
         V((STEPS, 3, 64, 128), bf16), V((STEPS, 4, 64, 128), bf16),
         V((STEPS, 2, 8, 128), f32), V((STEPS, 2, 8, 128), f32),
-        V((STEPS, 16, 128), bf16), V((STEPS, 16, n_col * 128), bf16),
-        V((STEPS, 64, 128), bf16), V((STEPS, 64, n_col * 128), bf16), V((8, 128), f32),
+        V((STEPS, 8, 128), bf16), V((STEPS, 8, n_col * 128), bf16),
+        V((STEPS, 64, 128), bf16), V((STEPS, 64, n_far * 128), bf16),
+        V((STEPS, GROUP, 64, 128), bf16), V((STEPS, GROUP, 64, 128), bf16),
+        V((8, 128), f32), V((GROUP, 8, 128), f32), V((GROUP, n_far * 128, 128), bf16),
         pltpu.SemaphoreType.DMA((STEPS * len(KINDS),)), pltpu.SemaphoreType.DMA((STEPS * len(KINDS),)),
-        pltpu.SemaphoreType.DMA((STEPS, 2, n_col)), pltpu.SemaphoreType.DMA((STEPS, 2, n_col)),
+        pltpu.SemaphoreType.DMA((STEPS, n_col)), pltpu.SemaphoreType.DMA((STEPS, n_col)),
+        pltpu.SemaphoreType.DMA((STEPS, n_far)), pltpu.SemaphoreType.DMA((STEPS, n_far)),
+        pltpu.SemaphoreType.DMA((STEPS, GROUP)), pltpu.SemaphoreType.DMA((STEPS, GROUP)),
+        pltpu.SemaphoreType.DMA((GROUP,)), pltpu.SemaphoreType.DMA((GROUP,)),
         pltpu.SemaphoreType.DMA((22,)),
     ]
     operands = (

time: 81.6 us -> 53.3 us (0.65)
  the two profiles are of different devices: /device:TPU:1 before, /device:TPU:497 now
where the time goes in v2:
time: 53.3 us; the launch traced here: 53.1 us
  Pallas kernels  49.8 us (93%)
  local copies, waits for them, and re-layouts  2.7 us (5%)
  between operations  0.65 us (1%)
    pallas_call x1, Pallas kernels, shards(): pl.pallas_call(kernel, name='coupled', out_shape=(jax.ShapeDtypeStruct((2...  49.8 us
    unnamed x4, local copies, waits for them, and re-layouts  2.7 us

profile of v2, /device:TPU:497, one launch (start us, length us, event | category | flops | bytes accessed | tf_op | source)
XLA Modules:
  0.0 53.1 jit_solution(8227420420146539496)
XLA Ops:
  0.6 49.8 %coupled.1 = (bf16[2400,128]{1,0:T(8,128)(2,1)S(1)}, f32[480,128]{1,0:T(8,128)S(1)}, f32[8,128]{1,0:T(8,128)S(1)}, f32[3,4,128]{2,1,0:T(4,128)S(1)}) custom-call(bf16[2400,128]{1,0:T(8,128)(2,1)} %bitcast.15, f32[2,4,128]{2,1,0:T(4,128)} %refs_1_.1, f32[3,4,128]{2,1,0:T(4,128)} %refs_2_.1, s32[4,128]{1,0:T(4,128)} %refs_3_.1, bf16[600,600]{1,0:T(8,128)(2,1)} %refs_4_.1, ...), custom_call_target="tpu_custom_call" | custom-call | tf_op jit(solution)/shard_map/coupled/pallas_call | solution.py:650
  50.4 0.8 %copy.30 = bf16[600,4,128]{2,1,0:T(4,128)(2,1)} copy(bf16[600,4,128]{2,1,0:T(4,128)(2,1)S(1)} %bitcast.13) | data formatting | bytes 1228800
  51.2 0.7 %copy.31 = f32[2,30,8,128]{3,2,1,0:T(8,128)} copy(f32[2,30,8,128]{3,2,1,0:T(8,128)S(1)} %bitcast.14) | data formatting | bytes 491520
  51.9 0.6 %copy.32 = f32[8,128]{1,0:T(8,128)} copy(f32[8,128]{1,0:T(8,128)S(1)} %get-tuple-element.18) | data formatting | bytes 8192
  52.5 0.6 %copy.33 = f32[3,4,128]{2,1,0:T(4,128)} copy(f32[3,4,128]{2,1,0:T(4,128)S(1)} %get-tuple-element.19) | data formatting | bytes 12288

commit v3 on v2

--- a/solution.py
+++ b/solution.py
@@ -39,6 +39,14 @@
     high = x.astype(bf16)
     low = (x - high.astype(f32)).astype(bf16)
     return high, low
+
+
+def deliver(*refs):
+    copies = [pltpu.make_async_copy(refs[i], refs[4 + i], refs[8].at[i]) for i in range(4)]
+    for copy in copies:
+        copy.start()
+    for copy in copies:
+        copy.wait()
 
 
 def kernel(
@@ -54,12 +62,12 @@
     ) = local
     (
     wide, energy, transfer, maps16, mall, proj, speed, cos_s, windbuf, curbuf, wwet8,
-    whot, ohot, idxbuf, fhot,
+    whot, ohot, idxbuf,
     rows_s, tpose, mixp, kmat, coef, orow, fw, vw, kv, forc, keys, backv, forced, smooth,
     sel, ins,
     slot_send, slot_recv, key_send, key_recv, bulk_send, bulk_recv, back_send, back_recv,
-    kf_send, kf_all, line_send, lines, chosen_send, chosen_all, index_send, index_all, lhot,
-    ssem, rsem, fs_sem, fr_sem, far_s, far_r, near_s, near_r, index_s, index_r, lsem,
+    kf_send, kf_all, kn_send, kn_all, line_send, lines, chosen_send, chosen_all, index_send, index_all, lhot,
+    ssem, rsem, fs_sem, fr_sem, ks_sem, kr_sem, far_s, far_r, near_s, near_r, index_s, index_r, lsem,
     ) = refs
     n_row, n_col = lax.axis_size("row"), lax.axis_size("col")
     row, col = lax.axis_index("row"), lax.axis_index("col")
@@ -71,6 +79,9 @@
     top = row == n_row - 1
     bottom = row == 0
     barrier = pltpu.get_barrier_semaphore()
+    n_far = n_col // GROUP
+    far_block = col // GROUP
+    member = lax.rem(col, GROUP)
 
     def peer(i):
         return lax.rem(col + i, n_col)
@@ -90,11 +101,18 @@
 
     @pl.when(top)
     def _():
-        def tell(i, carry):
-            signal_to((row, peer(i)))
-            return carry
-
-        lax.fori_loop(1, n_col, tell, 0)
+        for i in range(1, n_far):
+            signal_to((row, peer(i * GROUP)))
+        for i in range(1, GROUP):
+            signal_to((row, far_block * GROUP + lax.rem(member + i, GROUP)))
+
+        @pl.when(member == 0)
+        def _():
+            signal_to(west)
+
+        @pl.when(member == GROUP - 1)
+        def _():
+            signal_to(east)
 
     loads = [pltpu.make_async_copy(src, dst, lsem.at[i]) for i, (src, dst) in enumerate(zip(inputs, local))]
     early = (1, 2, 3, 5, 6, 7, 8, 18)
@@ -117,26 +135,24 @@
             device_id=at[way], device_id_type=MESH,
         )
 
-    n_far = n_col // GROUP
-    far_block = col // GROUP
-    member = lax.rem(col, GROUP)
 
     def lanes_of(i):
         return pl.ds(pl.multiple_of(i * 128, 128), 128)
 
-    def key_copy(step, i, sender):
+    def key_far(step, i, sender):
         return pltpu.make_async_remote_copy(
             src_ref=kf_send.at[step], dst_ref=kf_all.at[step, :, lanes_of(sender)],
             send_sem=fs_sem.at[step, i], recv_sem=fr_sem.at[step, sender],
-            device_id=(row, peer(i)), device_id_type=MESH,
+            device_id=(row, peer(i * GROUP)), device_id_type=MESH,
         )
 
-    def key_fold(step, act, receiving=False):
-        def one(i, carry):
-            act(key_copy(step, i, peer(i) if receiving else col))
-            return carry
-
-        lax.fori_loop(1, n_col, one, 0)
+    def key_near(step, i, sender):
+        other = far_block * GROUP + lax.rem(member + i, GROUP)
+        return pltpu.make_async_remote_copy(
+            src_ref=kn_send.at[step, i], dst_ref=kn_all.at[step, sender],
+            send_sem=ks_sem.at[step, i], recv_sem=kr_sem.at[step, sender],
+            device_id=(row, other), device_id_type=MESH,
+        )
 
     def far_copy(step, i, sender):
         return pltpu.make_async_remote_copy(
@@ -266,9 +282,13 @@
     def _():
         pl.semaphore_wait(barrier, 3)
 
-    @pl.when(top)
-    def _():
-        pl.semaphore_wait(barrier, n_col)
+    @pl.when(top & ((member == 0) | (member == GROUP - 1)))
+    def _():
+        pl.semaphore_wait(barrier, n_far + GROUP)
+
+    @pl.when(top & (member > 0) & (member < GROUP - 1))
+    def _():
+        pl.semaphore_wait(barrier, n_far + GROUP - 1)
 
     def each(msgs, act, receiving):
         for way, copy in msgs:
@@ -355,11 +375,6 @@
     ins[...] = jnp.where(cell_t == edge_t, 1.0, 0.0).astype(bf16)
 
     ohot[...] = one_hot(osend_ref, 1024)
-
-    @pl.when(top)
-    def _():
-        hot = iota((n_col * 128, 128), 0) == fold_ref[...]
-        fhot[...] = jnp.where(hot, 1.0, 0.0).astype(bf16)
 
     def prepare_ocean(step):
         kv[...] = jnp.dot(kmat[:, 0:64], vw[...], precision=highest, preferred_element_type=f32)
@@ -430,14 +445,16 @@
             edges = jnp.where(lane8 == y, pltpu.roll(keys[y], y + 1, 1), edges)
             edges = jnp.where(lane8 == 8 + y, pltpu.roll(keys[y], 8 + y, 1), edges)
         key_send[step, 2] = edges
-        msgs = start(step, "key")
 
         @pl.when(top)
         def _():
             line = keys[7].astype(bf16)
             kf_send[step] = line
-            kf_all[step, :, lanes_of(col)] = line
-            key_fold(step, lambda copy: copy.start())
+            kf_all[step, :, lanes_of(far_block)] = line
+            for i in range(1, n_far):
+                key_far(step, i, far_block).start()
+
+        msgs = start(step, "key")
 
         force = forc[...]
         for c, gain in enumerate((gain_u, gain_v)):
@@ -457,12 +474,6 @@
             lines[step, :, lanes_of(far_block)] = line
             for i in range(1, n_far):
                 far_copy(step, i, far_block).start()
-
-        return msgs, bulks
-
-    def select_lines(step):
-        @pl.when(top)
-        def _():
             if step == 0:
                 for i in range(1, GROUP):
                     index_copy(i, lax.rem(member + i, GROUP)).wait_recv()
@@ -471,6 +482,12 @@
                 for i in range(GROUP):
                     wanted = index_all[lax.rem(member + i, GROUP)][0:1, :].astype(jnp.int32)
                     lhot[i] = jnp.where(column == wanted, 1.0, 0.0).astype(bf16)
+
+        return msgs, bulks
+
+    def select_lines(step):
+        @pl.when(top)
+        def _():
             for i in range(1, n_far):
                 far_copy(step, i, lax.rem(far_block + i, n_far)).wait_recv()
             for i in range(GROUP):
@@ -482,12 +499,29 @@
                     near_copy(step, i, near_part).start()
 
     def finish_keys(step, msgs):
-        wait_for(msgs)
 
         @pl.when(top)
         def _():
-            key_fold(step, lambda copy: copy.wait_recv(), True)
-            key_recv[step, 1] = -jnp.dot(kf_all[step], fhot[...], preferred_element_type=f32)
+            for i in range(1, n_far):
+                key_far(step, i, lax.rem(far_block + i, n_far)).wait_recv()
+            for i in list(range(1, GROUP)) + [0]:
+                chosen = jnp.dot(kf_all[step], lhot[i], preferred_element_type=f32).astype(bf16)
+                if i == 0:
+                    kn_all[step, member] = chosen
+                else:
+                    kn_send[step, i] = chosen
+                    key_near(step, i, member).start()
+
+        wait_for(msgs)
+
+        @pl.when(top)
+        def _():
+            for i in range(1, GROUP):
+                key_near(step, i, lax.rem(member + i, GROUP)).wait_recv()
+            total = kn_all[step, 0].astype(f32)
+            for i in range(1, GROUP):
+                total = total + kn_all[step, i].astype(f32)
+            key_recv[step, 1] = -total
 
         south_halo = jnp.where(bottom, 0.0, key_recv[step, 0])
         north_halo = key_recv[step, 1]
@@ -594,11 +628,12 @@
     @pl.when(top)
     def _():
         for step in range(STEPS):
-            key_fold(step, lambda copy: copy.wait_send())
             for i in range(1, n_far):
+                key_far(step, i, far_block).wait_send()
                 far_copy(step, i, far_block).wait_send()
             for i in range(1, GROUP):
                 near_copy(step, i, near_part).wait_send()
+                key_near(step, i, member).wait_send()
         for i in range(1, GROUP):
             index_copy(i, member).wait_send()
 
@@ -617,7 +652,7 @@
         V((2400, 128), f32), V((STEPS, SPEC, 512), bf16), V((SPEC, 512), f32), V((16, SPEC), f32),
         V((416, SPEC), bf16), V((208, 512), f32), V((NDIR, 512), f32), V((2, NDIR, 128), f32),
         V((8, 512), f32), V((8, 512), f32), V((8, 512), f32),
-        V((512, 384), bf16), V((1024, 384), bf16), V((1, 384), jnp.int32), V((n_col * 128, 128), bf16),
+        V((512, 384), bf16), V((1024, 384), bf16), V((1, 384), jnp.int32),
         V((8, 128), f32), V((128, 128), f32), V((32, 32), f32), V((8, 128), f32), V((4, 8, 128), f32),
         V((1, 1024), f32), V((8, 1024), f32), V((64, 1024), f32), V((8, 1024), f32), V((8, 1024), f32),
         V((8, 8, 128), f32), V((8, 1024), f32), V((64, 1024), f32), V((64, 1024), f32),
@@ -626,12 +661,14 @@
         V((STEPS, 3, 8, 128), f32), V((STEPS, 4, 8, 128), f32),
         V((STEPS, 3, 64, 128), bf16), V((STEPS, 4, 64, 128), bf16),
         V((STEPS, 2, 8, 128), f32), V((STEPS, 2, 8, 128), f32),
-        V((STEPS, 8, 128), bf16), V((STEPS, 8, n_col * 128), bf16),
+        V((STEPS, 8, 128), bf16), V((STEPS, 8, n_far * 128), bf16),
+        V((STEPS, GROUP, 8, 128), bf16), V((STEPS, GROUP, 8, 128), bf16),
         V((STEPS, 64, 128), bf16), V((STEPS, 64, n_far * 128), bf16),
         V((STEPS, GROUP, 64, 128), bf16), V((STEPS, GROUP, 64, 128), bf16),
         V((8, 128), f32), V((GROUP, 8, 128), f32), V((GROUP, n_far * 128, 128), bf16),
         pltpu.SemaphoreType.DMA((STEPS * len(KINDS),)), pltpu.SemaphoreType.DMA((STEPS * len(KINDS),)),
-        pltpu.SemaphoreType.DMA((STEPS, n_col)), pltpu.SemaphoreType.DMA((STEPS, n_col)),
+        pltpu.SemaphoreType.DMA((STEPS, n_far)), pltpu.SemaphoreType.DMA((STEPS, n_far)),
+        pltpu.SemaphoreType.DMA((STEPS, GROUP)), pltpu.SemaphoreType.DMA((STEPS, GROUP)),
         pltpu.SemaphoreType.DMA((STEPS, n_far)), pltpu.SemaphoreType.DMA((STEPS, n_far)),
         pltpu.SemaphoreType.DMA((STEPS, GROUP)), pltpu.SemaphoreType.DMA((STEPS, GROUP)),
         pltpu.SemaphoreType.DMA((GROUP,)), pltpu.SemaphoreType.DMA((GROUP,)),
@@ -663,6 +700,16 @@
             collective_id=0, has_side_effects=True, vmem_limit_bytes=40 * 1024 * 1024
         ),
     )(*[pltpu.with_memory_space_constraint(x, pltpu.HBM) for x in operands])
+    done = (spec_out, vel_out, eta_out, cur_out)
+    spec_out, vel_out, eta_out, cur_out = pl.pallas_call(
+        deliver,
+        name="deliver",
+        out_shape=tuple(jax.ShapeDtypeStruct(x.shape, x.dtype) for x in done),
+        in_specs=[vmem] * 4,
+        out_specs=(hbm,) * 4,
+        scratch_shapes=[pltpu.SemaphoreType.DMA((4,))],
+        compiler_params=pltpu.CompilerParams(vmem_limit_bytes=4 * 1024 * 1024),
+    )(*done)
     return (
         spec_out.reshape(SPEC, 4, 128),
         vel_out.reshape(2, LEV, 8, 128),

time: 53.3 us -> 49.9 us (0.936)
  local copies, waits for them, and re-layouts: 2.7 us -> 0 us
  Pallas kernels: 49.8 us -> 49.1 us
    unnamed x4 -> x0, local copies, waits for them, and re-layouts: 2.7 us -> none
    pallas_call x1, Pallas kernels: 49.8 us -> 48.2 us  [shards(): pl.pallas_call(kernel, name='coupled', out_shape=(jax.ShapeDtypeStruct((2...]
    pallas_call x0 -> x1, Pallas kernels: none -> 0.94 us  [shards(): pl.pallas_call(deliver, name='deliver', out_shape=tuple((jax.ShapeDtypeSt...]
where the time goes in v3:
time: 49.9 us; the launch traced here: 49.7 us
  Pallas kernels  49.1 us (98%)
  between operations  0.65 us (1%)
    pallas_call x1, Pallas kernels, shards(): pl.pallas_call(kernel, name='coupled', out_shape=(jax.ShapeDtypeStruct((2...  48.2 us

profile of v3, /device:TPU:497, one launch (start us, length us, event | category | flops | bytes accessed | tf_op | source)
XLA Modules:
  0.0 49.7 jit_solution(10785207862704445125)
XLA Ops:
  0.6 48.2 %coupled.1 = (bf16[2400,128]{1,0:T(8,128)(2,1)S(1)}, f32[480,128]{1,0:T(8,128)S(1)}, f32[8,128]{1,0:T(8,128)S(1)}, f32[3,4,128]{2,1,0:T(4,128)S(1)}) custom-call(bf16[2400,128]{1,0:T(8,128)(2,1)} %bitcast.13, f32[2,4,128]{2,1,0:T(4,128)} %refs_1_.1, f32[3,4,128]{2,1,0:T(4,128)} %refs_2_.1, s32[4,128]{1,0:T(4,128)} %refs_3_.1, bf16[600,600]{1,0:T(8,128)(2,1)} %refs_4_.1, ...), custom_call_target="tpu_custom_call" | custom-call | tf_op jit(solution)/shard_map/coupled/pallas_call | solution.py:687
  48.8 0.9 %deliver.1 = (bf16[2400,128]{1,0:T(8,128)(2,1)}, f32[480,128]{1,0:T(8,128)}, f32[8,128]{1,0:T(8,128)}, f32[3,4,128]{2,1,0:T(4,128)}) custom-call(bf16[2400,128]{1,0:T(8,128)(2,1)S(1)} %get-tuple-element.12.refs_0_, f32[480,128]{1,0:T(8,128)S(1)} %get-tuple-element.13.refs_1_, f32[8,128]{1,0:T(8,128)S(1)} %get-tuple-element.14.refs_2_, ...), custom_call_target="tpu_custom_call" | custom-call | tf_op jit(solution)/shard_map/deliver/pallas_call | solution.py:704

commit v4 on v3

--- a/solution.py
+++ b/solution.py
@@ -25,6 +25,11 @@
 
 KINDS = (
     ("slot", "n"), ("slot", "s"),
+    ("more", "n2"), ("more", "s2"), ("more", "e"), ("more", "w"),
+    ("more", "ne"), ("more", "nw"), ("more", "se"), ("more", "sw"),
+    ("wide", "n"), ("wide", "s"), ("wide", "e"), ("wide", "w"),
+    ("mask", "n"), ("mask", "s"), ("mask", "e"), ("mask", "w"),
+    ("line", "n"), ("line", "s"), ("line", "e"), ("line", "w"),
     ("key", "n"), ("key", "s"), ("key", "e"), ("key", "w"),
     ("bulk", "n"), ("bulk", "s"), ("bulk", "e"), ("bulk", "w"),
     ("back", "n"), ("back", "s"),
@@ -65,7 +70,8 @@
     whot, ohot, idxbuf,
     rows_s, tpose, mixp, kmat, coef, orow, fw, vw, kv, forc, keys, backv, forced, smooth,
     sel, ins,
-    slot_send, slot_recv, key_send, key_recv, bulk_send, bulk_recv, back_send, back_recv,
+    slot_send, slot_recv, more_send, more_recv, wide_l, wide_es, wide_e, mask_es, mask_r, line_es, line_r, edge_f,
+    key_send, key_recv, bulk_send, bulk_recv, back_send, back_recv,
     kf_send, kf_all, kn_send, kn_all, line_send, lines, chosen_send, chosen_all, index_send, index_all, lhot,
     ssem, rsem, fs_sem, fr_sem, ks_sem, kr_sem, far_s, far_r, near_s, near_r, index_s, index_r, lsem,
     ) = refs
@@ -75,9 +81,16 @@
     south = (lax.rem(row + n_row - 1, n_row), col)
     east = (row, lax.rem(col + 1, n_col))
     west = (row, lax.rem(col + n_col - 1, n_col))
-    at = {"n": north, "s": south, "e": east, "w": west}
+    up, down = lax.rem(row + 1, n_row), lax.rem(row + n_row - 1, n_row)
+    right, left = lax.rem(col + 1, n_col), lax.rem(col + n_col - 1, n_col)
+    at = {
+        "n": north, "s": south, "e": east, "w": west,
+        "ne": (up, right), "nw": (up, left), "se": (down, right), "sw": (down, left),
+        "n2": (lax.rem(row + 2, n_row), col), "s2": (lax.rem(row + n_row - 2, n_row), col),
+    }
     top = row == n_row - 1
     bottom = row == 0
+    near_top, near_bottom = row >= n_row - 2, row <= 1
     barrier = pltpu.get_barrier_semaphore()
     n_far = n_col // GROUP
     far_block = col // GROUP
@@ -91,11 +104,21 @@
 
     @pl.when(jnp.logical_not(bottom))
     def _():
-        signal_to(south)
+        for way in ("s", "se", "sw"):
+            signal_to(at[way])
+
+    @pl.when(jnp.logical_not(near_bottom))
+    def _():
+        signal_to(at["s2"])
+
+    @pl.when(jnp.logical_not(near_top))
+    def _():
+        signal_to(at["n2"])
 
     @pl.when(jnp.logical_not(top))
     def _():
-        signal_to(north)
+        for way in ("n", "ne", "nw"):
+            signal_to(at[way])
         signal_to(east)
         signal_to(west)
 
@@ -121,9 +144,22 @@
 
     def message(step, kind, way):
         place = step * len(KINDS) + KINDS.index((kind, way))
-        index = {"n": 0, "s": 1, "e": 2, "w": 3}[way]
+        index = {"n": 0, "s": 1, "e": 2, "w": 3, "n2": 4, "s2": 5, "ne": 6, "nw": 7, "se": 8, "sw": 9}[way]
+        line = slice(7 * 128, 8 * 128) if way == "n" else slice(0, 128)
         if kind == "slot":
             src, dst = slot_send.at[step, index], slot_recv.at[step, index]
+        elif kind == "more":
+            part = {"n": 2, "s": 0, "e": 1, "w": 1}[way[0]]
+            src, dst = more_send.at[part], more_recv.at[index]
+        elif kind == "wide":
+            if index < 2:
+                src, dst = orecv_v.at[:, line], wide_l.at[index]
+            else:
+                src, dst = wide_es, wide_e.at[index - 2]
+        elif kind == "mask":
+            src, dst = fw.at[:, line] if index < 2 else mask_es, mask_r.at[index]
+        elif kind == "line":
+            src, dst = kv.at[:, line] if index < 2 else line_es, line_r.at[index]
         elif kind == "key":
             src, dst = key_send.at[step, min(index, 2)], key_recv.at[step, index]
         elif kind == "bulk":
@@ -267,32 +303,35 @@
             total = total + speed[k : k + 1, :] * proj[8 * k : 8 * k + 8, :]
         fields = (total * wwet8[...]).astype(bf16)
         slots = jnp.dot(fields, whot[...], preferred_element_type=f32)
-        slot_send[step, 1] = slots[:, 0:128]
-        slot_send[step, 0] = slots[:, 256:384]
+        for index, j in ((1, 0), (0, 2)):
+            slot_send[step, index, 0:8] = slots[:, j * 128 : (j + 1) * 128]
+            slot_send[step, index, 8:16] = slots[:, 128:256]
+        if step == 1:
+            for j in range(3):
+                more_send[j] = slots[:, j * 128 : (j + 1) * 128]
         return slots[:, 128 : 128 + SLOT].astype(bf16)
 
     project(0)
     own_slots = send_slots(0)
 
-    @pl.when(jnp.logical_not(top | bottom))
-    def _():
-        pl.semaphore_wait(barrier, 4)
-
-    @pl.when(bottom)
-    def _():
-        pl.semaphore_wait(barrier, 3)
-
-    @pl.when(top & ((member == 0) | (member == GROUP - 1)))
-    def _():
-        pl.semaphore_wait(barrier, n_far + GROUP)
-
-    @pl.when(top & (member > 0) & (member < GROUP - 1))
-    def _():
-        pl.semaphore_wait(barrier, n_far + GROUP - 1)
+    is_top = lax.div(row + 1, n_row)
+    is_border = lax.div(member + 1, GROUP) + 1 - lax.div(member + GROUP - 1, GROUP)
+    partners = (
+        3 * (1 - is_top)
+        + 3 * lax.div(row + n_row - 1, n_row)
+        + (1 - lax.div(row + 2, n_row))
+        + lax.div(row + n_row - 2, n_row)
+        + 2 * (1 - is_top)
+        + is_top * (n_far + GROUP - 2 + is_border)
+    )
+    pl.semaphore_wait(barrier, partners)
 
     def each(msgs, act, receiving):
         for way, copy in msgs:
-            edge = {"n": bottom if receiving else top, "s": top if receiving else bottom}.get(way)
+            high, low, high2, low2 = top, bottom, near_top, near_bottom
+            if receiving:
+                high, low, high2, low2 = bottom, top, near_bottom, near_top
+            edge = {"n": high, "s": low, "n2": high2, "s2": low2}.get(way if way[-1] == "2" else way[0])
             if edge is None:
                 act(copy)
             else:
@@ -339,6 +378,7 @@
     rows_s[5:6, 0:LEV] = thick_ref[...]
     mixp[...] = jnp.zeros_like(mixp)
     mixp[0:LEV, 0:LEV] = mix_ref[...]
+    mixp[32:64, :] = pltpu.roll(mixp[0:32, :], 32, 1)
 
     def wide_row(i):
         return jnp.broadcast_to(rows_s[i : i + 1, :], (8, 128))
@@ -357,13 +397,18 @@
     gain_u = turned[0:32, 0:8]
     gain_v = turned[0:32, 8:16]
     m0, thick = wide_row(0), wide_row(5)
-    for i, (profile, weight) in enumerate(((along_u, m0), (along_v, m0), (along_u, thick), (along_v, thick))):
-        coef[i] = jnp.broadcast_to(jnp.sum(profile * weight, axis=1, keepdims=True), (8, 128))
     m0_far = pltpu.roll(m0, 32, 1)
     thick_far = pltpu.roll(thick, 32, 1)
-    kmat[...] = jnp.where(
+    base = jnp.where(
         r8 == 0, m0, jnp.where(r8 == 1, m0_far, jnp.where(r8 == 2, thick, jnp.where(r8 == 3, thick_far, 0.0)))
     )
+    mixed = jnp.dot(base[:, 0:64], mixp[...], precision=highest, preferred_element_type=f32)
+    kmat[...] = jnp.where(r8 < 4, base, pltpu.roll(mixed, 4, 0))
+    m0_mix = jnp.broadcast_to(kmat[4:5, :], (8, 128))
+    thick_mix = jnp.broadcast_to(kmat[6:7, :], (8, 128))
+    for i, weight in enumerate((m0, thick, m0_mix, thick_mix)):
+        for c, profile in enumerate((along_u, along_v)):
+            coef[2 * i + c] = jnp.broadcast_to(jnp.sum(profile * weight, axis=1, keepdims=True), (8, 128))
 
     cell = iota((1024, 128), 0)
     spot = iota((1024, 128), 1)
@@ -378,6 +423,14 @@
 
     def prepare_ocean(step):
         kv[...] = jnp.dot(kmat[:, 0:64], vw[...], precision=highest, preferred_element_type=f32)
+        if step == 1:
+
+            @pl.when(top)
+            def _():
+                added = viscous * orow[0:1, 7 * 128 : 8 * 128] * pltpu.roll(key_recv[0, 1], 4, 0)
+                kv[:, 7 * 128 : 8 * 128] = kv[:, 7 * 128 : 8 * 128] + jnp.where(r8 < 4, added, 0.0)
+
+            start_more(1)
 
     loads[9].wait()
     vw[...] = jnp.zeros_like(vw)
@@ -418,11 +471,80 @@
     update_energy(0)
     loads[19].wait()
     loads[21].wait()
+    def side_columns(tiles):
+        edges = jnp.zeros((8, 128), f32)
+        for y in range(8):
+            edges = jnp.where(lane8 == y, pltpu.roll(tiles[y], y + 1, 1), edges)
+            edges = jnp.where(lane8 == 8 + y, pltpu.roll(tiles[y], 8 + y, 1), edges)
+        return edges
+
+    fixed_msgs, line_msgs = [], []
+
+    def start_fixed():
+        spot16, cell16 = iota((16, 1024), 0), iota((16, 1024), 1)
+        edge16 = jnp.where(spot16 < 8, spot16 * 128 + 127, (spot16 - 8) * 128)
+        pick = jnp.where(cell16 == edge16, 1.0, 0.0).astype(bf16)
+        wide_es[...] = lax.dot_general(
+            pick, orecv_v[...], (((1,), (1,)), ((), ())), preferred_element_type=f32
+        ).astype(bf16)
+        mask_es[...] = side_columns([fw[:, y * 128 : (y + 1) * 128] for y in range(8)])
+        fixed_msgs.extend(start(0, "mask") + start(0, "wide"))
+
+    def start_more(step):
+        line_es[...] = side_columns([kv[:, y * 128 : (y + 1) * 128] for y in range(8)])
+        line_msgs.extend(start(step, "line"))
+
+    def halo_key(force, index):
+        force = force * mask_r[index]
+        value = line_r[index]
+        for i in range(4):
+            extra = jnp.sum(force * coef[i], axis=0, keepdims=True)
+            value = value + jnp.where(r8 == i, extra, 0.0)
+        key_recv[1, index] = value
+
+    def finish_more():
+        wait_for(fixed_msgs)
+        wait_for(more_msgs)
+        wait_for(line_msgs)
+
+        def slots_of(ref, off):
+            return jnp.where(off, 0.0, ref[:, 0:SLOT]).astype(bf16)
+
+        def product(parts, weights):
+            total = jnp.dot(parts[0], weights[0:64, :], preferred_element_type=f32)
+            for j in (1, 2):
+                total = total + jnp.dot(parts[j], weights[j * 64 : j * 64 + 64, :], preferred_element_type=f32)
+            return total
+
+        own = [more_send[j][:, 0:SLOT].astype(bf16) for j in range(3)]
+        south_mid = slots_of(slot_recv.at[1, 0, 8:16], bottom)
+        north_mid = slots_of(slot_recv.at[1, 1, 8:16], top)
+        halo_key(product((own[0], south_mid, slots_of(more_recv.at[4], near_bottom)), wide_l.at[0]), 0)
+
+        @pl.when(jnp.logical_not(top))
+        def _():
+            halo_key(product((slots_of(more_recv.at[5], near_top), north_mid, own[2]), wide_l.at[1]), 1)
+
+        for index, high, low in ((2, 8, 6), (3, 9, 7)):
+            parts = (
+                slots_of(more_recv.at[high], top),
+                more_recv[index][:, 0:SLOT].astype(bf16),
+                slots_of(more_recv.at[low], bottom),
+            )
+            total = jnp.zeros((8, 16), f32)
+            for j in range(3):
+                total = total + lax.dot_general(
+                    parts[j], wide_e[index - 2][:, j * 64 : j * 64 + 64], (((1,), (1,)), ((), ())),
+                    preferred_element_type=f32,
+                )
+            edge_f[...] = jnp.zeros_like(edge_f)
+            edge_f[:, 0:16] = total
+            halo_key(edge_f[...], index)
 
     def pass_north(step, own_slots, slot_msgs):
         wait_for(slot_msgs)
-        from_south = jnp.where(bottom, 0.0, slot_recv[step, 0][:, 0:SLOT]).astype(bf16)
-        from_north = jnp.where(top, 0.0, slot_recv[step, 1][:, 0:SLOT]).astype(bf16)
+        from_south = jnp.where(bottom, 0.0, slot_recv[step, 0][0:8, 0:SLOT]).astype(bf16)
+        from_north = jnp.where(top, 0.0, slot_recv[step, 1][0:8, 0:SLOT]).astype(bf16)
         force = (
             jnp.dot(from_north, orecv_v[0:64, :], preferred_element_type=f32)
             + jnp.dot(own_slots, orecv_v[64:128, :], preferred_element_type=f32)
@@ -434,17 +556,10 @@
             lanes = slice(y * 128, (y + 1) * 128)
             tile = force[:, lanes]
             value = kv[:, lanes]
-            for i in range(4):
+            for i in range(8 if y == 7 and step == 0 else 4):
                 extra = jnp.sum(tile * coef[i], axis=0, keepdims=True)
                 value = value + jnp.where(r8 == i, extra, 0.0)
             keys[y] = value
-        key_send[step, 0] = keys[7]
-        key_send[step, 1] = keys[0]
-        edges = jnp.zeros((8, 128), f32)
-        for y in range(8):
-            edges = jnp.where(lane8 == y, pltpu.roll(keys[y], y + 1, 1), edges)
-            edges = jnp.where(lane8 == 8 + y, pltpu.roll(keys[y], 8 + y, 1), edges)
-        key_send[step, 2] = edges
 
         @pl.when(top)
         def _():
@@ -454,8 +569,15 @@
             for i in range(1, n_far):
                 key_far(step, i, far_block).start()
 
-        msgs = start(step, "key")
-
+        msgs = []
+        if step == 0:
+            key_send[step, 0] = keys[7]
+            key_send[step, 1] = keys[0]
+            key_send[step, 2] = side_columns([keys[y] for y in range(8)])
+            msgs = start(step, "key")
+
+        if step == 1:
+            fold_fix(0)
         force = forc[...]
         for c, gain in enumerate((gain_u, gain_v)):
             forced[c * 32 : c * 32 + 32, :] = vw[c * 32 : c * 32 + 32, :] + jnp.dot(
@@ -512,7 +634,10 @@
                     kn_send[step, i] = chosen
                     key_near(step, i, member).start()
 
-        wait_for(msgs)
+        if step == 0:
+            wait_for(msgs)
+        else:
+            finish_more()
 
         @pl.when(top)
         def _():
@@ -564,17 +689,8 @@
     def finish_velocity(step, bulks):
         wait_for(bulks)
 
-        @pl.when(top)
-        def _():
-            for i in range(1, GROUP):
-                near_copy(step, i, lax.rem(member + i, GROUP)).wait_recv()
-            total = chosen_all[step, 0].astype(f32)
-            for i in range(1, GROUP):
-                total = total + chosen_all[step, i].astype(f32)
-            bulk_recv[step, 1] = (-total).astype(bf16)
-
         south_halo = jnp.where(bottom, 0.0, bulk_recv[step, 0].astype(f32))
-        north_halo = bulk_recv[step, 1].astype(f32)
+        north_halo = jnp.where(top, 0.0, bulk_recv[step, 1].astype(f32))
         lane64 = iota((64, 128), 1)
         sides = jnp.where(lane64 < 8, bulk_recv[step, 2].astype(f32), bulk_recv[step, 3].astype(f32))
         outer = jnp.dot(sides.astype(bf16), ins[...], preferred_element_type=f32)
@@ -589,7 +705,7 @@
             smooth[:, lanes] = orow[0:1, lanes] * (here + viscous * around)
         for c in range(2):
             new = jnp.dot(
-                mixp[...], smooth[c * 32 : c * 32 + 32, :], precision=highest, preferred_element_type=f32
+                mixp[0:32, 0:32], smooth[c * 32 : c * 32 + 32, :], precision=highest, preferred_element_type=f32
             )
             if step == STEPS - 1:
                 for y in range(8):
@@ -597,32 +713,56 @@
             else:
                 vw[c * 32 : c * 32 + 32, :] = new * orow[0:1, :]
 
+    def fold_fix(step):
+        @pl.when(top)
+        def _():
+            for i in range(1, GROUP):
+                near_copy(step, i, lax.rem(member + i, GROUP)).wait_recv()
+            total = chosen_all[step, 0].astype(f32)
+            for i in range(1, GROUP):
+                total = total + chosen_all[step, i].astype(f32)
+            wet = orow[0:1, 7 * 128 : 8 * 128]
+            for c in range(2):
+                added = jnp.dot(
+                    mixp[0:32, 0:32], total[c * 32 : c * 32 + 32], precision=highest, preferred_element_type=f32
+                )
+                added = -viscous * wet * added
+                if step == STEPS - 1:
+                    spot = pl.ds(c * 8 * LEV + 7, LEV, stride=8)
+                    vel_out[spot, :] = vel_out[spot, :] + added[0:LEV]
+                else:
+                    rows = slice(c * 32, c * 32 + 32)
+                    vw[rows, 7 * 128 : 8 * 128] = vw[rows, 7 * 128 : 8 * 128] + added
+
     for step in range(STEPS):
         keys_sent, bulks = pass_north(step, own_slots, slot_msgs)
         pending += keys_sent + bulks
         if step == 0:
+            start_fixed()
+            pending += fixed_msgs
             project(1)
-        else:
-            update_energy(step)
         own_back, backs = finish_keys(step, keys_sent)
         pending += backs
         select_lines(step)
         if step == 0:
-            next_transfer(1)
+            finish_velocity(step, bulks)
+            prepare_ocean(1)
+            pending += line_msgs
         else:
-            pl.when(jnp.logical_not(top))(lambda: finish_velocity(step, bulks))
+            update_energy(step)
+            finish_velocity(step, bulks)
         finish_current(step, own_back, backs)
         if step == 0:
             speeds()
             own_slots = send_slots(1)
             slot_msgs = start(1, "slot")
-            pending += slot_msgs
-            finish_velocity(step, bulks)
-            prepare_ocean(1)
+            more_msgs = start(1, "more")
+            pending += slot_msgs + more_msgs
+            next_transfer(1)
     for y in range(4):
         for i in range(3):
             cur_out[i, y : y + 1, :] = curbuf[i : i + 1, y * 128 : (y + 1) * 128]
-    pl.when(top)(lambda: finish_velocity(STEPS - 1, bulks))
+    fold_fix(STEPS - 1)
     each(pending, lambda copy: copy.wait_send(), False)
 
     @pl.when(top)
@@ -653,11 +793,13 @@
         V((416, SPEC), bf16), V((208, 512), f32), V((NDIR, 512), f32), V((2, NDIR, 128), f32),
         V((8, 512), f32), V((8, 512), f32), V((8, 512), f32),
         V((512, 384), bf16), V((1024, 384), bf16), V((1, 384), jnp.int32),
-        V((8, 128), f32), V((128, 128), f32), V((32, 32), f32), V((8, 128), f32), V((4, 8, 128), f32),
+        V((8, 128), f32), V((128, 128), f32), V((64, 128), f32), V((8, 128), f32), V((8, 8, 128), f32),
         V((1, 1024), f32), V((8, 1024), f32), V((64, 1024), f32), V((8, 1024), f32), V((8, 1024), f32),
         V((8, 8, 128), f32), V((8, 1024), f32), V((64, 1024), f32), V((64, 1024), f32),
         V((1024, 128), bf16), V((128, 1024), bf16),
-        V((STEPS, 2, 8, 128), f32), V((STEPS, 2, 8, 128), f32),
+        V((STEPS, 2, 16, 128), f32), V((STEPS, 2, 16, 128), f32), V((3, 8, 128), f32), V((10, 8, 128), f32),
+        V((2, 192, 128), bf16), V((16, 192), bf16), V((2, 16, 192), bf16), V((8, 128), f32), V((4, 8, 128), f32),
+        V((8, 128), f32), V((4, 8, 128), f32), V((8, 128), f32),
         V((STEPS, 3, 8, 128), f32), V((STEPS, 4, 8, 128), f32),
         V((STEPS, 3, 64, 128), bf16), V((STEPS, 4, 64, 128), bf16),
         V((STEPS, 2, 8, 128), f32), V((STEPS, 2, 8, 128), f32),

time: 49.9 us -> 51 us (1.022)
  Pallas kernels: 49.1 us -> 50.2 us
    pallas_call x1, Pallas kernels: 48.2 us -> 49.2 us  [shards(): pl.pallas_call(kernel, name='coupled', out_shape=(jax.ShapeDtypeStruct((2...]
where the time goes in v4:
time: 51 us; the launch traced here: 50.8 us
  Pallas kernels  50.2 us (98%)
  between operations  0.65 us (1%)
    pallas_call x1, Pallas kernels, shards(): pl.pallas_call(kernel, name='coupled', out_shape=(jax.ShapeDtypeStruct((2...  49.2 us

profile of v4, /device:TPU:497, one launch (start us, length us, event | category | flops | bytes accessed | tf_op | source)
XLA Modules:
  0.0 50.8 jit_solution(13746335583992468310)
XLA Ops:
  0.6 49.2 %coupled.1 = (bf16[2400,128]{1,0:T(8,128)(2,1)S(1)}, f32[480,128]{1,0:T(8,128)S(1)}, f32[8,128]{1,0:T(8,128)S(1)}, f32[3,4,128]{2,1,0:T(4,128)S(1)}) custom-call(bf16[2400,128]{1,0:T(8,128)(2,1)} %bitcast.13, f32[2,4,128]{2,1,0:T(4,128)} %refs_1_.1, f32[3,4,128]{2,1,0:T(4,128)} %refs_2_.1, s32[4,128]{1,0:T(4,128)} %refs_3_.1, bf16[600,600]{1,0:T(8,128)(2,1)} %refs_4_.1, ...), custom_call_target="tpu_custom_call" | custom-call | tf_op jit(solution)/shard_map/coupled/pallas_call | solution.py:829
  49.9 0.9 %deliver.1 = (bf16[2400,128]{1,0:T(8,128)(2,1)}, f32[480,128]{1,0:T(8,128)}, f32[8,128]{1,0:T(8,128)}, f32[3,4,128]{2,1,0:T(4,128)}) custom-call(bf16[2400,128]{1,0:T(8,128)(2,1)S(1)} %get-tuple-element.12.refs_0_, f32[480,128]{1,0:T(8,128)S(1)} %get-tuple-element.13.refs_1_, f32[8,128]{1,0:T(8,128)S(1)} %get-tuple-element.14.refs_2_, ...), custom_call_target="tpu_custom_call" | custom-call | tf_op jit(solution)/shard_map/deliver/pallas_call | solution.py:846
